TPU v7x, 32 devices: a whole 2x2x4 slice. The times are simulated.
32 devices in a mesh: section: 2 (over core), dp: 16 (over z, y, x).
Axes of the slice: x: 2, y: 2, z: 4, core: 2. Of those that a mesh axis runs over, the one named last changes fastest.
Arguments:
- byte_states: bfloat16 [32768, 768], P('dp'), may hold values from -6 to 6
- lengths: int32 [32], P('dp'), may hold values from 512 to 1024, as said below
- patch_weight: bfloat16 [6144, 768], replicated, may hold values from -0.078125 to 0.078125
- qkv_weight: bfloat16 [2, 768, 2304], P('section'), may hold values from -0.21875 to 0.21875
- out_weight: bfloat16 [2, 768, 768], P('section'), may hold values from -0.875 to 0.875
- up_weight: bfloat16 [2, 768, 3072], P('section'), may hold values from -0.21875 to 0.21875
- down_weight: bfloat16 [2, 3072, 768], P('section'), may hold values from -0.109375 to 0.109375
- norm_gains: float32 [2, 2, 768], P('section'), may hold values from 0.25 to 1.75
- byte_cotangent: bfloat16 [32768, 768], P('dp'), may hold values from -6 to 6
Outputs:
- section_outputs: bfloat16 [2, 32768, 768], P('section', 'dp')
- input_grad: float32 [32768, 768], P('dp')
- patch_grad: float32 [6144, 768], P(('section', 'dp'))
- qkv_grad: float32 [2, 768, 2304], P('section', 'dp')
- proj_grad: float32 [2, 768, 768], P('section', 'dp')
- up_grad: float32 [2, 768, 3072], P('section', 'dp')
- down_grad: float32 [2, 3072, 768], P('section', 'dp')
- gain_grad: float32 [2, 2, 768], P('section', None, 'dp')
Inputs may be any that keep to these rules, and one draw needn't show every extreme that they name: `lengths`: each a multiple of 8; some sequence has all 1024 bytes live in every draw.
All inputs are finite; a program needn't handle non-finite values.
Results may differ from a plain program's by a relative error of at most 0.02.
Values may be sent and summed in bfloat16 or wider, within the bound.
A program may use at most 384 MiB of HBM per device.

v0:
```python
import jax
import jax.numpy as jnp
from jax import lax
from jax.sharding import PartitionSpec as P

D = 768
HEADS = 12
HDIM = 64
PATCH = 8
SEQ = 1024
MB = 2


def partner(value, axis, stride):
    mask = 2**stride
    pairs = [(source, source ^ mask) for source in range(lax.axis_size(axis))]
    return lax.ppermute(value, axis, pairs)


def product(left, right):
    return jnp.dot(left, right, preferred_element_type=jnp.float32)


def product_tn(left, right):
    return lax.dot_general(
        left, right, (((0,), (0,)), ((), ())), preferred_element_type=jnp.float32
    )


def product_nt(left, right):
    return lax.dot_general(
        left, right, (((1,), (1,)), ((), ())), preferred_element_type=jnp.float32
    )


def norm_scaled(hidden, gain):
    row_mean = jnp.mean(hidden, axis=-1, keepdims=True)
    centered = hidden - row_mean
    row_var = jnp.mean(centered * centered, axis=-1, keepdims=True)
    return centered * lax.rsqrt(row_var + 1e-05) * gain


def masked_softmax(scores):
    key_count = scores.shape[-1]
    allowed = jnp.arange(key_count)[:, None] >= jnp.arange(key_count)[None, :]
    return jax.nn.softmax(jnp.where(allowed, scores, -1e30), axis=-1)


def exact_gelu(values):
    return jax.nn.gelu(values, approximate=False)


def block_forward(hidden, weights, groups):
    w_qkv, w_out, w_up, w_down, gains = weights
    row_count = hidden.shape[0]
    normed = norm_scaled(hidden, gains[0]).astype(jnp.bfloat16)
    qkv = (
        product(normed, w_qkv)
        .astype(jnp.bfloat16)
        .reshape(groups, row_count // groups, 3, HEADS, HDIM)
    )
    query = qkv[:, :, 0]
    keys = qkv[:, :, 1]
    values = qkv[:, :, 2]
    scores = jnp.einsum(
        "blhe,bmhe->bhlm", query, keys, preferred_element_type=jnp.float32
    ) * HDIM ** (-0.5)
    probs_low = masked_softmax(scores).astype(jnp.bfloat16)
    attended = jnp.einsum("bhlm,bmhe->blhe", probs_low, values, preferred_element_type=jnp.float32)
    attended = attended.reshape(row_count, D).astype(jnp.bfloat16)
    middle = hidden + product(attended, w_out)
    normed_two = norm_scaled(middle, gains[1]).astype(jnp.bfloat16)
    pre_act = product(normed_two, w_up)
    active = exact_gelu(pre_act).astype(jnp.bfloat16)
    result = middle + product(active, w_down)
    saved = (
        hidden,
        normed,
        query,
        keys,
        values,
        scores,
        probs_low,
        attended,
        middle,
        normed_two,
        pre_act,
        active,
    )
    return (result, saved)


def block_backward(saved, grad_out, weights, groups):
    w_qkv, w_out, w_up, w_down, gains = weights
    (
        hidden,
        normed,
        query,
        keys,
        values,
        scores,
        probs_low,
        attended,
        middle,
        normed_two,
        pre_act,
        active,
    ) = saved
    row_count = hidden.shape[0]
    grad_branch = grad_out.astype(jnp.bfloat16)
    grad_down = product_tn(active, grad_branch)
    grad_active = product_nt(grad_branch, w_down)
    gelu_back = jax.vjp(exact_gelu, pre_act)[1]
    grad_pre = gelu_back(grad_active)[0].astype(jnp.bfloat16)
    grad_up = product_tn(normed_two, grad_pre)
    grad_normed_two = product_nt(grad_pre, w_up)
    norm_back_two = jax.vjp(norm_scaled, middle, gains[1])[1]
    grad_middle_part, grad_gain_two = norm_back_two(grad_normed_two)
    grad_middle = grad_out + grad_middle_part
    grad_attn_out = grad_middle.astype(jnp.bfloat16)
    grad_proj = product_tn(attended, grad_attn_out)
    grad_attended = product_nt(grad_attn_out, w_out).astype(jnp.bfloat16)
    grad_attended = grad_attended.reshape(groups, row_count // groups, HEADS, HDIM)
    grad_probs = jnp.einsum(
        "blhe,bmhe->bhlm", grad_attended, values, preferred_element_type=jnp.float32
    )
    grad_values = jnp.einsum(
        "bhlm,blhe->bmhe", probs_low, grad_attended, preferred_element_type=jnp.float32
    )
    soft_back = jax.vjp(masked_softmax, scores)[1]
    grad_scores = soft_back(grad_probs)[0].astype(jnp.bfloat16)
    grad_query = jnp.einsum(
        "bhlm,bmhe->blhe", grad_scores, keys, preferred_element_type=jnp.float32
    ) * HDIM ** (-0.5)
    grad_keys = jnp.einsum(
        "bhlm,blhe->bmhe", grad_scores, query, preferred_element_type=jnp.float32
    ) * HDIM ** (-0.5)
    grad_qkv = (
        jnp.stack([grad_query, grad_keys, grad_values], axis=2)
        .reshape(row_count, 3 * D)
        .astype(jnp.bfloat16)
    )
    grad_qkv_weight = product_tn(normed, grad_qkv)
    grad_normed = product_nt(grad_qkv, w_qkv)
    norm_back_one = jax.vjp(norm_scaled, hidden, gains[0])[1]
    grad_in_part, grad_gain_one = norm_back_one(grad_normed)
    grad_in = grad_middle + grad_in_part
    gradients = (
        grad_qkv_weight,
        grad_proj,
        grad_up,
        grad_down,
        jnp.stack([grad_gain_one, grad_gain_two]),
    )
    return (grad_in, gradients)


def global_forward(seq_input, patch_weight, weights):
    patches = seq_input.reshape(SEQ // PATCH, PATCH * D)
    projected = product(patches, patch_weight)
    shifted = jnp.concatenate([jnp.zeros((1, D), jnp.float32), projected[:-1]], axis=0)
    result, saved = block_forward(shifted, weights, 1)
    return (result.astype(jnp.bfloat16), saved, patches)


def global_backward(seq_input, grad_result, patch_weight, weights):
    outputs = global_forward(seq_input, patch_weight, weights)
    grad_shifted, gradients = block_backward(
        outputs[1], grad_result.astype(jnp.float32), weights, 1
    )
    grad_projected = jnp.concatenate(
        [grad_shifted[1:], jnp.zeros((1, D), jnp.float32)], axis=0
    ).astype(jnp.bfloat16)
    grad_patch_weight = product_tn(outputs[2], grad_projected)
    grad_patches = product_nt(grad_projected, patch_weight).reshape(SEQ, D)
    return (grad_patches, grad_patch_weight, gradients)


def local_pass(row_inputs, glob_rows, row_cotangents, live_rows, weights):
    row_count = row_inputs.shape[0]
    groups = row_count // PATCH
    spread = jnp.broadcast_to(
        glob_rows.astype(jnp.float32)[:, None, :], (groups, PATCH, D)
    ).reshape(row_count, D)
    result, saved = block_forward(row_inputs.astype(jnp.float32) + spread, weights, groups)
    local_out = (result * live_rows).astype(jnp.bfloat16)
    grad_in, gradients = block_backward(
        saved, row_cotangents.astype(jnp.float32) * live_rows, weights, groups
    )
    grad_glob = jnp.sum(grad_in.reshape(groups, PATCH, D), axis=1)
    return (local_out, grad_in, grad_glob, gradients)


def local_work(seq_input, glob_rows, seq_cotangent, seq_length, weights):
    live_rows = (jnp.arange(SEQ) < seq_length).astype(jnp.float32)[:, None]
    local_out, grad_in, grad_glob, gradients = local_pass(
        seq_input, glob_rows, seq_cotangent, live_rows, weights
    )
    return (local_out, grad_in, grad_glob, gradients)


def body(
    byte_states,
    lengths,
    patch_weight,
    qkv_weight,
    out_weight,
    up_weight,
    down_weight,
    norm_gains,
    byte_cotangent,
):
    weights = (qkv_weight[0], out_weight[0], up_weight[0], down_weight[0], norm_gains[0])
    seq_inputs = byte_states.reshape(MB, SEQ, D)
    seq_cotangents = byte_cotangent.reshape(MB, SEQ, D)
    patch_count = SEQ // PATCH
    zero_grads = tuple((jnp.zeros(weight.shape, jnp.float32) for weight in weights))
    section_first = lax.axis_index("section") == 0
    patch_total = jnp.zeros((PATCH * D, D), jnp.float32)
    input_parts = tuple((jnp.zeros((SEQ, D), jnp.float32) for position in range(MB)))
    section_parts = tuple((jnp.zeros((SEQ, D), jnp.bfloat16) for position in range(MB)))
    incoming = jnp.zeros((patch_count, D), jnp.bfloat16)
    totals = zero_grads
    for step_index in range(MB + 2):

        def early_work(patch_total, input_parts, section_parts, incoming, step_index=step_index):
            input_parts = list(input_parts)
            section_parts = list(section_parts)
            outgoing = jnp.zeros((patch_count, D), jnp.bfloat16)
            increment = zero_grads
            if step_index < MB:
                outgoing = global_forward(seq_inputs[step_index], patch_weight, weights)[0]
                section_parts[step_index] = jnp.broadcast_to(
                    outgoing[:, None, :], (patch_count, PATCH, D)
                ).reshape(SEQ, D)
            if step_index >= 2:
                earlier = step_index - 2
                grad_patches, grad_patch_weight, increment = global_backward(
                    seq_inputs[earlier], incoming, patch_weight, weights
                )
                patch_total = patch_total + grad_patch_weight
                input_parts[earlier] = input_parts[earlier] + grad_patches
            return (patch_total, tuple(input_parts), tuple(section_parts), outgoing, increment)

        def late_work(patch_total, input_parts, section_parts, incoming, step_index=step_index):
            input_parts = list(input_parts)
            section_parts = list(section_parts)
            outgoing = jnp.zeros((patch_count, D), jnp.bfloat16)
            increment = zero_grads
            if 1 <= step_index <= MB:
                current = step_index - 1
                local_out, grad_in, grad_glob, increment = local_work(
                    seq_inputs[current],
                    incoming,
                    seq_cotangents[current],
                    lengths[current],
                    weights,
                )
                section_parts[current] = local_out
                input_parts[current] = input_parts[current] + grad_in
                outgoing = grad_glob.astype(jnp.bfloat16)
            return (patch_total, tuple(input_parts), tuple(section_parts), outgoing, increment)

        patch_total, input_parts, section_parts, outgoing, increment = lax.cond(
            section_first, early_work, late_work, patch_total, input_parts, section_parts, incoming
        )
        if step_index <= MB:
            incoming = partner(outgoing, "section", 0)
        totals = tuple(jax.tree.map(jnp.add, totals, increment))
    reduced = (
        lax.psum_scatter(totals[0], "dp", scatter_dimension=0, tiled=True),
        lax.psum_scatter(totals[1], "dp", scatter_dimension=0, tiled=True),
        lax.psum_scatter(totals[2], "dp", scatter_dimension=0, tiled=True),
        lax.psum_scatter(totals[3], "dp", scatter_dimension=0, tiled=True),
        lax.psum_scatter(totals[4], "dp", scatter_dimension=1, tiled=True),
    )
    patch_grad = lax.psum_scatter(patch_total, ("section", "dp"), scatter_dimension=0, tiled=True)
    input_grad = lax.psum(
        jnp.concatenate(input_parts, axis=0).astype(jnp.bfloat16), "section"
    ).astype(jnp.float32)
    section_outputs = jnp.concatenate(section_parts, axis=0)[None]
    return (
        section_outputs,
        input_grad,
        patch_grad,
        reduced[0][None],
        reduced[1][None],
        reduced[2][None],
        reduced[3][None],
        reduced[4][None],
    )


def solution(mesh):
    return jax.shard_map(
        body,
        mesh=mesh,
        in_specs=(
            P("dp", None),
            P("dp"),
            P(),
            P("section", None, None),
            P("section", None, None),
            P("section", None, None),
            P("section", None, None),
            P("section", None, None),
            P("dp", None),
        ),
        out_specs=(
            P("section", "dp", None),
            P("dp", None),
            P(("section", "dp"), None),
            P("section", "dp", None),
            P("section", "dp", None),
            P("section", "dp", None),
            P("section", "dp", None),
            P("section", None, "dp"),
        ),
        check_vma=False,
    )
```

profile of v0, /device:TPU:8, one launch (start us, length us, event | category | flops | bytes accessed | tf_op | source)
XLA Modules:
  0.0 1767.1 jit_solution(11527721443098572360)
XLA Ops:
  8.1 23.1 %conditional.5 = (bf16[1024,768]{1,0:T(8,128)(2,1)}, bf16[128,768]{1,0:T(8,128)(2,1)}) conditional(s32[]{:T(128)} %convert_element_type.391, () %tuple.49, (bf16[2,1024,768]{2,1,0:T(8,128)(2,1)}, bf16[6144,768]{1,0:T(8,128)(2,1)}, f32[2,768]{1,0:T(2,128)}, bf16[768,2304]{1,0:T(8,128)(2,1)}, bf16[768,768]{1,0:T(8,128)(2,1)}, ...), branch_computations={%region_0.0_spmd, %region_1.8_spmd} | conditional | flops 3115567104 | bytes 61024328 | solution.py:264
  11.2 5.2 fusion.4
  19.7 9.2 fusion.16
  28.9 2.3 broadcast_bitcast_fusion
  32.8 42.9 %conditional.6 = (f32[1024,768]{1,0:T(8,128)}, bf16[1024,768]{1,0:T(8,128)(2,1)}, bf16[1024,768]{1,0:T(8,128)(2,1)}, bf16[128,768]{1,0:T(8,128)(2,1)S(1)}, f32[7...) conditional(s32[]{:T(128)} %convert_element_type.391, ...), branch_computations={%region_8.23_spmd, %region_23.30_spmd} | conditional | flops 43899658240 | bytes 609083392
  44.3 5.2 fusion.162
  52.9 8.5 convolution_add_fusion.3
  64.3 1.9 broadcast.1087
  66.6 4.7 broadcast_in_dim.197
  71.4 4.3 broadcast_in_dim.198
  75.7 252.4 %collective-permute-start.1 = (bf16[128,768]{1,0:T(8,128)(2,1)S(1)}, bf16[128,768]{1,0:T(8,128)(2,1)S(1)}, u32[]{:S(2)}, u32[]{:S(2)}) collective-permute-start(bf16[128,768]{1,0:T(8,128)(2,1)S(1)} %get-tuple-element.217), channel_id=1, source_target_pairs={{0,16},{16,0},{1,17},{17,1},{2,18},{18,2},{3,19},{19,3},{4,20},{20... | collective-permute-start | bytes 589832 | tf_op jit(solution)/shard_map/ppermute | solution.py:17
  329.2 104.0 %conditional.7 = (f32[6144,768]{1,0:T(8,128)}, f32[1024,768]{1,0:T(8,128)}, f32[1024,768]{1,0:T(8,128)}, bf16[1024,768]{1,0:T(8,128)(2,1)}, bf16[128,768]{1,0:T(...) conditional(s32[]{:T(128)} %convert_element_type.391, ...), branch_computations={%region_30.45_spmd, %region_45.59_spmd} | conditional | flops 43899658240 | bytes 626384768 | solution.py:264
  341.3 5.7 fusion.317
  350.1 3.3 fusion.351
  353.4 7.4 add_convert_fusion.2
  360.8 1.8 multiply_reduce_fusion.13
  365.4 1.7 fusion.331
  367.1 1.7 multiply_reduce_fusion.12
  369.7 1.9 multiply_reduce_fusion.14
  372.7 1.8 fusion.339
  374.5 4.8 fusion.336
  379.3 4.2 reshape.895
  383.6 4.9 add.257
  388.5 4.1 fusion.352
  392.5 6.9 fusion.332
  399.5 5.0 fusion.350
  404.5 7.9 convolution_bitcast_fusion
  412.4 18.7 %copy.173 = f32[6144,768]{1,0:T(8,128)} copy(f32[6144,768]{0,1:T(8,128)} %convolution_bitcast_fusion) | data formatting | bytes 37748736 | tf_op jit(solution)/shard_map
  431.1 2.0 broadcast.1201
  433.2 218.9 %collective-permute-start.2 = (bf16[128,768]{1,0:T(8,128)(2,1)S(1)}, bf16[128,768]{1,0:T(8,128)(2,1)S(1)}, u32[]{:S(2)}, u32[]{:S(2)}) collective-permute-start(bf16[128,768]{1,0:T(8,128)(2,1)S(1)} %get-tuple-element.224), channel_id=1, source_target_pairs={{0,16},{16,0},{1,17},{17,1},{2,18},{18,2},{3,19},{19,3},{4,20},{20... | collective-permute-start | bytes 589832 | tf_op jit(solution)/shard_map/ppermute | solution.py:17
  652.1 3.2 convert.58
  655.3 124.4 %conditional.8 = (f32[1024,768]{1,0:T(8,128)}, f32[768,2304]{1,0:T(8,128)}, f32[768,768]{1,0:T(8,128)}, f32[768,3072]{1,0:T(8,128)}, f32[3072,768]{1,0:T(8,128)}, /*index=5*/f32[2,768]{1,0:T(2,128)}, f32[6144,768]{1,0:T(8,128)}) conditional(s32[]{:T(128)} %convert_element_type.391, (f32[6144,768]{1,0:T(8,128)}, f32[1024,768]{1,0:T(8,128)}) %tuple.55, ...), branch_computations={%region_59.60_spmd, %region_60.74_spmd} | conditional | flops 8667383808 | bytes 363947360 | solution.py:264
  657.3 2.7 slice.140
  659.9 3.7 squeeze.48
  663.7 5.6 fusion.356
  675.3 3.3 fusion.390
  678.7 7.4 add_convert_fusion.3
  686.1 1.8 multiply_reduce_fusion.20
  692.4 1.7 multiply_reduce_fusion.19
  695.0 1.7 multiply_reduce_fusion.21
  697.8 1.8 fusion.378
  699.7 4.8 fusion.375
  704.4 4.2 reshape.903
  708.7 5.0 add.268
  713.7 4.0 fusion.391
  717.7 7.0 fusion.371
  724.7 5.1 fusion.389
  729.8 18.8 %copy.181 = f32[6144,768]{0,1:T(8,128)} copy(f32[6144,768]{1,0:T(8,128)} %get-tuple-element.328) | data formatting | bytes 37748736 | tf_op jit(solution)/shard_map
  748.6 12.2 bitcast_add_fusion
  760.8 18.7 %copy.200 = f32[6144,768]{1,0:T(8,128)} copy(f32[6144,768]{0,1:T(8,128)} %bitcast_add_fusion) | data formatting | bytes 37748736 | tf_op jit(solution)/shard_map/cond | solution.py:264
  779.8 2.2 convert.59
  783.7 1.9 pad_maximum_fusion.6
  787.2 4.2 add_add_fusion.15
  791.5 12.8 add_add_fusion.14
  804.4 16.5 add_add_fusion.13
  821.0 14.0 add_add_fusion.12
  835.6 3.8 maximum_bitcast_fusion
  839.4 67.0 %reduce-scatter.19.cloned.1.call-done = f32[48,2]{1,0:T(8,128)} async-done(((f32[768,2]{1,0:T(8,128)}), f32[48,2]{1,0:T(8,128)}) %reduce-scatter.19.cloned.1.call-update) | async-done | bytes 400
  907.8 5.1 convert_element_type.393
  912.9 125.9 %reduce-scatter.13.cloned.1.call-done = f32[48,768]{1,0:T(8,128)} async-done(((f32[768,768]{1,0:T(8,128)}), f32[48,768]{1,0:T(8,128)}) %reduce-scatter.13.cloned.1.call-update) | async-done | bytes 147472 | tf_op jit(solution)/shard_map/reduce_scatter | solution.py:272
  1038.8 155.8 %reduce-scatter.11.cloned.1.call-done = f32[48,2304]{1,0:T(8,128)} async-done(((f32[768,2304]{1,0:T(8,128)}), f32[48,2304]{1,0:T(8,128)}) %reduce-scatter.11.cloned.1.call-update) | async-done | bytes 442384 | tf_op jit(solution)/shard_map/reduce_scatter | solution.py:271
  1194.6 176.7 %reduce-scatter.15.cloned.1.call-done = f32[48,3072]{1,0:T(8,128)} async-done(((f32[768,3072]{1,0:T(8,128)}), f32[48,3072]{1,0:T(8,128)}) %reduce-scatter.15.cloned.1.call-update) | async-done | bytes 589840 | tf_op jit(solution)/shard_map/reduce_scatter | solution.py:273
  1371.2 176.0 %reduce-scatter.17.cloned.1.call-done = f32[192,768]{1,0:T(8,128)} async-done(((f32[3072,768]{1,0:T(8,128)}), f32[192,768]{1,0:T(8,128)}) %reduce-scatter.17.cloned.1.call-update) | async-done | bytes 589840 | tf_op jit(solution)/shard_map/reduce_scatter | solution.py:274
  1547.2 212.0 %reduce-scatter.9.cloned.1.call-done = f32[192,768]{1,0:T(8,128)} async-done(((f32[6144,768]{1,0:T(8,128)}), f32[192,768]{1,0:T(8,128)}) %reduce-scatter.9.cloned.1.call-update) | async-done | bytes 589840 | tf_op jit(solution)/shard_map/reduce_scatter | solution.py:277
  (264 shorter events, 49.4 us)
Async XLA Ops:
  8.0 898.4 %reduce-scatter.19.cloned.1.call-start = ((), (), s32[]{:S(2)}) async-start(), calls=%async_computation.12 | async-start | bytes 417792
  8.1 24.8 %copy-start.133 = (s32[2]{0:T(128)S(1)}, s32[2]{0:T(128)}, u32[]{:S(2)}) copy-start(s32[2]{0:T(128)} %param.18) | copy-start | bytes 28
  11.2 5.6 copy-start.1
  31.2 1.7 collective-permute-start
  44.3 5.6 copy-start.4
  61.3 4.8 copy-start.94
  71.4 4.3 copy-start.95
  75.7 253.5 %copy-start.58 = (f32[768,2304]{1,0:T(8,128)}, f32[768,2304]{1,0:T(8,128)S(1)}, u32[]{:S(2)}) copy-start(f32[768,2304]{1,0:T(8,128)S(1)} %get-tuple-element.227) | copy-start | bytes 21233668
  75.7 253.5 %copy-start.123 = (f32[2,768]{1,0:T(2,128)}, f32[2,768]{1,0:T(2,128)S(1)}, u32[]{:S(2)}) copy-start(f32[2,768]{1,0:T(2,128)S(1)} %get-tuple-element.239) | copy-start | bytes 18436
  75.7 253.5 %collective-permute-start.1 = (bf16[128,768]{1,0:T(8,128)(2,1)S(1)}, bf16[128,768]{1,0:T(8,128)(2,1)S(1)}, u32[]{:S(2)}, u32[]{:S(2)}) collective-permute-start(bf16[128,768]{1,0:T(8,128)(2,1)S(1)} %get-tuple-element.217), channel_id=1, source_target_pairs={{0,16},{16,0},{1,17},{17,1},{2,18},{18,2},{3,19},{19,3},{4,20},{20... | collective-permute-start | bytes 589832 | tf_op jit(solution)/shard_map/ppermute | solution.py:17
  341.3 5.7 copy-start.39
  341.3 6.1 copy-start.7
  348.8 4.6 copy-start.72
  349.2 4.2 copy-start.87
  350.0 3.4 copy-start.92
  350.0 10.8 slice-start.6
  353.4 7.4 copy-start.81
  353.4 7.4 slice-start.7
  360.8 1.8 copy-start.68
  362.6 11.9 slice-start
  364.2 4.6 copy-start.73
  365.4 3.6 copy-start.78
  365.4 4.3 copy-start.8
  367.1 7.5 slice-start.1
  369.7 3.0 copy-start.88
  369.7 4.8 slice-start.2
  388.4 4.1 copy-start.82
  388.4 4.1 copy-start.93
  392.5 6.9 copy-start.69
  399.5 5.0 copy-start.40
  433.2 222.1 %copy-start = (bf16[1,768,2304]{2,1,0:T(8,128)(2,1)S(1)}, bf16[1,768,2304]{2,1,0:T(8,128)(2,1)}, u32[]{:S(2)}) copy-start(bf16[1,768,2304]{2,1,0:T(8,128)(2,1)} %param.20) | copy-start | bytes 10616836
  433.2 222.1 %copy-start.96 = (f32[1,2,768]{2,1,0:T(2,128)S(1)}, f32[1,2,768]{2,1,0:T(2,128)}, u32[]{:S(2)}) copy-start(f32[1,2,768]{2,1,0:T(2,128)} %param.24) | copy-start | bytes 18436
  433.2 222.1 %collective-permute-start.2 = (bf16[128,768]{1,0:T(8,128)(2,1)S(1)}, bf16[128,768]{1,0:T(8,128)(2,1)S(1)}, u32[]{:S(2)}, u32[]{:S(2)}) collective-permute-start(bf16[128,768]{1,0:T(8,128)(2,1)S(1)} %get-tuple-element.224), channel_id=1, source_target_pairs={{0,16},{16,0},{1,17},{17,1},{2,18},{18,2},{3,19},{19,3},{4,20},{20... | collective-permute-start | bytes 589832 | tf_op jit(solution)/shard_map/ppermute | solution.py:17
  655.3 14.7 copy-start.9
  671.6 3.0 copy-start.20
  671.6 3.0 copy-start.38
  674.3 4.3 copy-start.74
  674.6 4.1 copy-start.89
  675.3 3.4 copy-start.98
  675.3 10.8 slice-start.8
  678.7 7.4 copy-start.83
  678.7 7.4 slice-start.9
  686.1 1.8 copy-start.70
  687.9 11.8 slice-start.3
  688.3 5.8 copy-start.108
  689.5 4.6 copy-start.75
  690.6 3.6 copy-start.80
  690.7 4.3 copy-start.10
  692.3 7.3 slice-start.4
  694.9 2.4 copy-start.132
  695.0 2.8 copy-start.90
  695.0 4.7 slice-start.5
  713.7 4.0 copy-start.84
  713.7 4.0 copy-start.99
  717.7 7.0 copy-start.71
  729.8 18.8 %copy-start.41 = (bf16[128,6144]{1,0:T(8,128)(2,1)S(1)}, bf16[128,6144]{1,0:T(8,128)(2,1)}, u32[]{:S(2)}) copy-start(bf16[128,6144]{1,0:T(8,128)(2,1)} %squeeze.48) | copy-start | bytes 4718596 | tf_op jit(solution)/shard_map/cond
  779.7 2.2 copy-start.124
  779.7 3.9 copy-start.61
  783.6 124.1 %all-reduce.8.cloned.1.call-start = ((), (), s32[]{:S(2)}) async-start(), calls=%async_computation.6 | async-start | bytes 6291456 | tf_op jit(solution)/shard_map/psum | solution.py:278
  785.6 253.2 %reduce-scatter.13.cloned.1.call-start = ((), (), s32[]{:S(2)}) async-start(), calls=%async_computation.9 | async-start | bytes 2506752 | tf_op jit(solution)/shard_map/reduce_scatter | solution.py:272
  791.5 403.1 %reduce-scatter.11.cloned.1.call-start = ((), (), s32[]{:S(2)}) async-start(), calls=%async_computation.8 | async-start | bytes 7520256 | tf_op jit(solution)/shard_map/reduce_scatter | solution.py:271
  804.4 566.9 %reduce-scatter.15.cloned.1.call-start = ((), (), s32[]{:S(2)}) async-start(), calls=%async_computation.10 | async-start | bytes 10027008 | tf_op jit(solution)/shard_map/reduce_scatter | solution.py:273
  821.0 726.3 %reduce-scatter.17.cloned.1.call-start = ((), (), s32[]{:S(2)}) async-start(), calls=%async_computation.11 | async-start | bytes 10027008 | tf_op jit(solution)/shard_map/reduce_scatter | solution.py:274
  835.1 924.1 %reduce-scatter.9.cloned.1.call-start = ((), (), s32[]{:S(2)}) async-start(), calls=%async_computation.7 | async-start | bytes 19464192 | tf_op jit(solution)/shard_map/reduce_scatter | solution.py:277
  (10 other events, 10.7 us)
Sparse Core Ops, SparseCore 0:
  783.8 122.5 reduce-scatter.18
  911.9 126.8 reduce-scatter.12
  1045.6 148.9 reduce-scatter.10
  1201.6 169.5 reduce-scatter.14
  1377.3 169.8 reduce-scatter.16
  1555.2 203.9 reduce-scatter.8
Sparse Core Ops, SparseCore 1:
  787.0 24.4 all-reduce.7
where the time goes:
time: 1780 us; the launch traced here: 1770 us
  waiting for transfers between devices  917 us (52%)
  starting transfers between devices  472 us (27%)
  matrix products  153 us (9%)
  local copies, waits for them, and re-layouts  110 us (6%)
  other arithmetic  80.9 us (5%)
  loops' own time  18.9 us (1%)
    ppermute x3, starting transfers between devices, partner(): return lax.ppermute(value, axis, pairs)  471 us
    reduce_scatter x1, waiting for transfers between devices, body(): lax.psum_scatter(patch_total, ('section', 'dp'), scatter_dimension=0, til...  212 us
    reduce_scatter x1, waiting for transfers between devices, body(): lax.psum_scatter(totals[2], 'dp', scatter_dimension=0, tiled=True)  177 us
    reduce_scatter x1, waiting for transfers between devices, body(): lax.psum_scatter(totals[3], 'dp', scatter_dimension=0, tiled=True)  176 us
    reduce_scatter x1, waiting for transfers between devices, body(): lax.psum_scatter(totals[0], 'dp', scatter_dimension=0, tiled=True)  156 us
    reduce_scatter x1, waiting for transfers between devices, body(): lax.psum_scatter(totals[1], 'dp', scatter_dimension=0, tiled=True)  126 us
    unnamed x8, waiting for transfers between devices  67.6 us
    dot_general x10, matrix products, product_tn(): lax.dot_general(left, right, (((0,), (0,)), ((), ())), preferred_element_...  55.9 us
  transfers between devices with their start and end apart: 10, of which 8 were waited for; matrix products, arithmetic and copies ran while one was open for 4% of the time, Pallas kernels for 0%

commit v1 on v0

v1 whole, which is shorter than its diff:
```python
import functools

import jax
import jax.numpy as jnp
from jax import lax
from jax.experimental import pallas as pl
from jax.experimental.pallas import tpu as pltpu
from jax.sharding import PartitionSpec as P

D = 768
HEADS = 12
HDIM = 64
FF = 3072
PATCH = 8
SEQ = 1024
PATCHES = SEQ // PATCH
TILE = 256
SUBS = TILE // 128
PAIRS = HEADS // 2
TILES = SEQ // TILE
MB = 2
XG = 3 * D + FF
F32 = jnp.float32
BF16 = jnp.bfloat16
ANY = pl.BlockSpec(memory_space=pl.ANY)
VLIMIT = 56 * 2**20


def sds(shape, dtype):
    return jax.ShapeDtypeStruct(shape, dtype)


def mm(a, b):
    return jnp.dot(a, b, preferred_element_type=F32)


def mm_nt(a, b):
    return lax.dot_general(a, b, (((1,), (1,)), ((), ())), preferred_element_type=F32)


def mm_tn(a, b):
    return lax.dot_general(a, b, (((0,), (0,)), ((), ())), preferred_element_type=F32)


def normalized(v):
    centered = v - jnp.mean(v, axis=-1, keepdims=True)
    scale = lax.rsqrt(jnp.mean(centered * centered, axis=-1, keepdims=True) + 1e-5)
    return centered * scale, scale


def norm_backward(grad, gain, hat, scale):
    scaled = grad * gain
    inner = scaled - jnp.mean(scaled, axis=-1, keepdims=True)
    inner = inner - hat * jnp.mean(scaled * hat, axis=-1, keepdims=True)
    return inner * scale, jnp.sum(grad * hat, axis=0, keepdims=True)


def gelu_pair(z):
    t = 1.0 / (1.0 + 0.3275911 * 0.7071067811865476 * jnp.abs(z))
    bell = jnp.exp(-0.5 * z * z)
    poly = 1.061405429 * t - 1.453152027
    poly = poly * t + 1.421413741
    poly = poly * t - 0.284496736
    poly = poly * t + 0.254829592
    half_tail = 0.5 * poly * t * bell
    cdf = jnp.where(z >= 0, 1.0 - half_tail, half_tail)
    return z * cdf, cdf + z * bell * 0.3989422804014327


def lane_masks():
    lane = lax.broadcasted_iota(jnp.int32, (128, 128), 1)
    first = jnp.where(lane < HDIM, 1.0, 0.0)
    return first.astype(BF16), (1.0 - first).astype(BF16), lane < HDIM


def split_heads(v, first, second):
    return jnp.concatenate([v * first, v * second], axis=0)


def attention_forward(qkv_ref, o_ref, p_ref, shift):
    first, second, _ = lane_masks()
    row = lax.broadcasted_iota(jnp.int32, (128, 256), 0)
    col = lax.broadcasted_iota(jnp.int32, (128, 256), 1) & 127
    allowed = (col <= row) & ((col >> shift) == (row >> shift))
    for sub in range(SUBS):
        rows = slice(sub * 128, sub * 128 + 128)
        for pair in range(PAIRS):
            lo = pair * 128
            q = qkv_ref[rows, lo : lo + 128]
            k2 = split_heads(qkv_ref[rows, D + lo : D + lo + 128], first, second)
            v2 = split_heads(qkv_ref[rows, 2 * D + lo : 2 * D + lo + 128], first, second)
            s = jnp.where(allowed, mm_nt(q, k2) * 0.125, -1e30)
            parts = []
            for half in range(2):
                sh = s[:, half * 128 : half * 128 + 128]
                e = jnp.exp(sh - jnp.max(sh, axis=-1, keepdims=True))
                parts.append(e / jnp.sum(e, axis=-1, keepdims=True))
            p = jnp.concatenate(parts, axis=1).astype(BF16)
            p_ref[sub, pair] = p
            o_ref[rows, lo : lo + 128] = mm(p, v2).astype(BF16)


def attention_backward(qkv_ref, p_ref, do_ref, dqkv_ref):
    first, second, is_first = lane_masks()
    for sub in range(SUBS):
        rows = slice(sub * 128, sub * 128 + 128)
        for pair in range(PAIRS):
            lo = pair * 128
            q = qkv_ref[rows, lo : lo + 128]
            k2 = split_heads(qkv_ref[rows, D + lo : D + lo + 128], first, second)
            v2 = split_heads(qkv_ref[rows, 2 * D + lo : 2 * D + lo + 128], first, second)
            do = do_ref[rows, lo : lo + 128]
            p = p_ref[sub, pair]
            dp = mm_nt(do, v2)
            pf = p.astype(F32)
            weighted = pf * dp
            parts = []
            for half in range(2):
                cols = slice(half * 128, half * 128 + 128)
                total = jnp.sum(weighted[:, cols], axis=-1, keepdims=True)
                parts.append(weighted[:, cols] - pf[:, cols] * total)
            ds = jnp.concatenate(parts, axis=1).astype(BF16)
            dq = mm(ds, k2) * 0.125
            dk2 = mm_tn(ds, q) * 0.125
            dv2 = mm_tn(p, do)
            dk = jnp.where(is_first, dk2[:128], dk2[128:])
            dv = jnp.where(is_first, dv2[:128], dv2[128:])
            dqkv_ref[rows, lo : lo + 128] = dq.astype(BF16)
            dqkv_ref[rows, D + lo : D + lo + 128] = dk.astype(BF16)
            dqkv_ref[rows, 2 * D + lo : 2 * D + lo + 128] = dv.astype(BF16)


def block_forward(h, gains, w, wait, shift, a_ref, qkv_ref, p_ref, o_ref, mid_ref, c_ref, u_ref, gp_ref):
    wq, wo, wu, wd = w
    a_ref[...] = (normalized(h)[0] * gains[0:1, :]).astype(BF16)
    wait(0)
    for part in range(3):
        cols = slice(part * D, part * D + D)
        qkv_ref[:, cols] = mm(a_ref[...], wq[:, cols]).astype(BF16)
    attention_forward(qkv_ref, o_ref, p_ref, shift)
    wait(1)
    mid = h + mm(o_ref[...], wo[...])
    mid_ref[...] = mid
    c_ref[...] = (normalized(mid)[0] * gains[1:2, :]).astype(BF16)
    wait(2)
    for part in range(FF // D):
        cols = slice(part * D, part * D + D)
        u, gp = gelu_pair(mm(c_ref[...], wu[:, cols]))
        u_ref[:, cols] = u.astype(BF16)
        gp_ref[:, cols] = gp.astype(BF16)
    wait(3)
    return mid_ref[...] + mm(u_ref[...], wd[...])


def block_backward(dout, h, gains, w, wait, dz_ref, mid_ref, qkv_ref, p_ref, do_ref, dr_ref, dqkv_ref):
    wq, wo, wu = w
    hat, scale = normalized(mid_ref[...])
    wait(2)
    dc = mm_nt(dz_ref[...], wu[...])
    back, dgain_two = norm_backward(dc, gains[1:2, :], hat, scale)
    dmid = dout + back
    dr_ref[...] = dmid.astype(BF16)
    wait(1)
    do_ref[...] = mm_nt(dr_ref[...], wo[...]).astype(BF16)
    attention_backward(qkv_ref, p_ref, do_ref, dqkv_ref)
    wait(0)
    da = mm_nt(dqkv_ref[...], wq[...])
    hat, scale = normalized(h)
    back, dgain_one = norm_backward(da, gains[0:1, :], hat, scale)
    return dmid + back, jnp.concatenate([dgain_one, dgain_two], axis=0)


LANES = D // 128


def fill_lanes(dst, src):
    for b in range(LANES):
        dst[b] = src[:, b * 128 : b * 128 + 128].astype(F32)


def strided_rows(ref, start, rows):
    picked = [ref[b, pl.ds(start, rows, stride=PATCH), :] for b in range(LANES)]
    return jnp.concatenate(picked, axis=1)


def spread_matrix():
    row = lax.broadcasted_iota(jnp.int32, (TILE, TILE // PATCH), 0) // PATCH
    col = lax.broadcasted_iota(jnp.int32, (TILE, TILE // PATCH), 1)
    return jnp.where(row == col, 1.0, 0.0).astype(BF16)


def cost(flops, nbytes):
    return pl.CostEstimate(flops=int(flops), bytes_accessed=int(nbytes), transcendentals=0)


WSCRATCH = {
    "q": pltpu.VMEM((D, 3 * D), BF16),
    "o": pltpu.VMEM((D, D), BF16),
    "u": pltpu.VMEM((D, FF), BF16),
    "d": pltpu.VMEM((FF, D), BF16),
}


def global_forward_kernel(
    scal, bytes_ref, gains_ref, wp_hbm, wq_hbm, wo_hbm, wu_hbm, wd_hbm,
    g_ref, x_ref, start_ref, qkv_ref, p_ref, mid_ref, gp_ref,
    bytes_f32, wp, wq, wo, wu, wd, psem, wsem,
):
    @pl.when(scal[0] == 0)
    def _():
        pcopies = [
            pltpu.make_async_copy(wp_hbm.at[pl.ds(j * D, D)], wp.at[pl.ds(j * D, D)], psem.at[j])
            for j in range(PATCH)
        ]
        wcopies = [
            pltpu.make_async_copy(src.at[0], dst, wsem.at[i])
            for i, (src, dst) in enumerate(((wq_hbm, wq), (wo_hbm, wo), (wu_hbm, wu), (wd_hbm, wd)))
        ]
        for copy in pcopies + wcopies:
            copy.start()
        fill_lanes(bytes_f32, bytes_ref)
        rows = MB * PATCHES
        acc = jnp.zeros((rows, D), F32)
        for j in range(PATCH):
            xj = strided_rows(bytes_f32, j, rows).astype(BF16)
            pcopies[j].wait()
            acc = acc + mm(xj, wp[j * D : j * D + D, :])
        moved = pltpu.roll(acc, 1, 0)
        row = lax.broadcasted_iota(jnp.int32, (rows, D), 0)
        start_ref[...] = jnp.where((row & (PATCHES - 1)) == 0, 0.0, moved)
        out = block_forward(
            start_ref[...], gains_ref[0], (wq, wo, wu, wd), lambda i: wcopies[i].wait(), 7,
            x_ref.at[:, 0:D], qkv_ref, p_ref, x_ref.at[:, D : 2 * D], mid_ref,
            x_ref.at[:, 2 * D : 3 * D], x_ref.at[:, 3 * D : 3 * D + FF], gp_ref,
        )
        g_ref[...] = out.astype(BF16)


def global_forward(scal, states, gains, patch_weight, weights):
    rows = MB * PATCHES
    full = lambda *shape: pl.BlockSpec(shape, lambda i, s: (0,) * len(shape), pipeline_mode=pl.Buffered(1))
    outs = (
        ((rows, D), BF16), ((rows, XG), BF16), ((rows, D), F32), ((rows, 3 * D), BF16),
        ((SUBS, PAIRS, 128, 256), BF16), ((rows, D), F32), ((rows, FF), BF16),
    )
    return pl.pallas_call(
        global_forward_kernel,
        name="global_forward",
        out_shape=[sds(*o) for o in outs],
        grid_spec=pltpu.PrefetchScalarGridSpec(
            num_scalar_prefetch=1,
            grid=(1,),
            in_specs=[full(MB * SEQ, D), full(1, 2, D)] + [ANY] * 5,
            out_specs=[full(*o[0]) for o in outs],
            scratch_shapes=[
                pltpu.VMEM((LANES, MB * SEQ, 128), F32), pltpu.VMEM((PATCH * D, D), BF16),
                WSCRATCH["q"], WSCRATCH["o"], WSCRATCH["u"], WSCRATCH["d"],
                pltpu.SemaphoreType.DMA((PATCH,)), pltpu.SemaphoreType.DMA((4,)),
            ],
        ),
        compiler_params=pltpu.CompilerParams(vmem_limit_bytes=VLIMIT),
        cost_estimate=cost(6e9, 32e6),
    )(scal, states, gains, patch_weight, *weights)


def global_backward_kernel(
    scal, dg0_ref, dg1_ref, start_ref, mid_ref, qkv_ref, p_ref, gp_ref, gains_ref, wq_hbm, wo_hbm, wu_hbm, wd_hbm,
    dpp_ref, keep_ref, send_ref, dgain_ref,
    dm_s, dz_s, do_s, dr_s, dqkv_s, wq, wo, wu, wd, wsem,
):
    @pl.when(scal[0] == 0)
    def _():
        rows = MB * PATCHES
        wcopies = [
            pltpu.make_async_copy(src.at[0], dst, wsem.at[i])
            for i, (src, dst) in enumerate(((wq_hbm, wq), (wo_hbm, wo), (wu_hbm, wu), (wd_hbm, wd)))
        ]
        for i in (3, 2, 1, 0):
            wcopies[i].start()
        dm_s[0:PATCHES, :] = dg0_ref[...]
        dm_s[PATCHES:, :] = dg1_ref[...]
        wcopies[3].wait()
        for part in range(FF // D):
            cols = slice(part * D, part * D + D)
            du = mm_nt(dm_s[...], wd[cols, :])
            dz_s[:, cols] = (du * gp_ref[:, cols].astype(F32)).astype(BF16)
        dh, dgain = block_backward(
            dm_s[...].astype(F32), start_ref[...], gains_ref[0], (wq, wo, wu), lambda i: wcopies[i].wait(),
            dz_s, mid_ref, qkv_ref, p_ref, do_s, dr_s, dqkv_s,
        )
        dgain_ref[...] = jnp.zeros_like(dgain_ref)
        dgain_ref[0:2, :] = dgain
        moved = pltpu.roll(dh, rows - 1, 0)
        row = lax.broadcasted_iota(jnp.int32, (rows, D), 0)
        dpp_ref[...] = jnp.where((row & (PATCHES - 1)) == PATCHES - 1, 0.0, moved).astype(BF16)
        for half in range(2):
            def fill(ref):
                lo = 0
                for src, width in ((dqkv_s, 3 * D // 2), (dr_s, D // 2), (dz_s, FF // 2), (dm_s, D // 2)):
                    ref[:, lo : lo + width] = src[:, half * width : half * width + width]
                    lo += width
            pl.when(scal[1] == half)(functools.partial(fill, keep_ref))
            pl.when(scal[1] != half)(functools.partial(fill, send_ref))

    @pl.when(scal[0] != 0)
    def _():
        dgain_ref[...] = jnp.zeros_like(dgain_ref)


def global_backward(scal, dgs, saved, gains, weights):
    rows = MB * PATCHES
    full = lambda *shape: pl.BlockSpec(shape, lambda i, s: (0,) * len(shape), pipeline_mode=pl.Buffered(1))
    width = (3 * D + D + FF + D) // 2
    outs = (((rows, D), BF16), ((rows, width), BF16), ((rows, width), BF16), ((8, D), F32))
    return pl.pallas_call(
        global_backward_kernel,
        name="global_backward",
        out_shape=[sds(*o) for o in outs],
        grid_spec=pltpu.PrefetchScalarGridSpec(
            num_scalar_prefetch=1,
            grid=(1,),
            in_specs=[full(PATCHES, D)] * 2 + [full(*v.shape) for v in saved] + [full(1, 2, D)] + [ANY] * 4,
            out_specs=[full(*o[0]) for o in outs],
            scratch_shapes=[
                pltpu.VMEM((rows, D), BF16), pltpu.VMEM((rows, FF), BF16), pltpu.VMEM((rows, D), BF16),
                pltpu.VMEM((rows, D), BF16), pltpu.VMEM((rows, 3 * D), BF16),
                WSCRATCH["q"], WSCRATCH["o"], WSCRATCH["u"], WSCRATCH["d"],
                pltpu.SemaphoreType.DMA((4,)),
            ],
        ),
        compiler_params=pltpu.CompilerParams(vmem_limit_bytes=VLIMIT),
        cost_estimate=cost(6e9, 24e6),
    )(scal, *dgs, *saved, gains, *weights)


def start_weights(scal, pairs, sems, order):
    step = pl.program_id(0)
    for i in order:
        own, recv, dst = pairs[i]

        @pl.when((step == 0) & (scal[0] == 1))
        def _(own=own, dst=dst, i=i):
            pltpu.make_async_copy(own.at[0], dst, sems.at[i]).start()

        @pl.when((step == 0) & (scal[0] == 0))
        def _(recv=recv, dst=dst, i=i):
            pltpu.make_async_copy(recv.at[0], dst, sems.at[i]).start()

    def wait(i):
        @pl.when(step == 0)
        def _():
            pltpu.make_async_copy(pairs[i][1].at[0], pairs[i][2], sems.at[i]).wait()

    return wait


def live_rows(scal):
    step = pl.program_id(0)
    row = lax.broadcasted_iota(jnp.int32, (TILE, D), 0) + step * TILE
    return row < scal[4]


def local_forward_kernel(
    scal, bytes_ref, cot_ref, g_ref, gains_ref, wq_a, wo_a, wu_a, wd_a, wq_b, wo_b, wu_b, wd_b, gains_b,
    y_ref, dm_ref, a_ref, qkv_ref, p_ref, o_ref, mid_ref, c_ref, u_ref, gp_ref,
    wq, wo, wu, wd, wsem,
):
    pairs = ((wq_a, wq_b, wq), (wo_a, wo_b, wo), (wu_a, wu_b, wu), (wd_a, wd_b, wd))
    wait = start_weights(scal, pairs, wsem, (0, 1, 2, 3))
    gains = jnp.where(scal[0] == 1, gains_ref[0], gains_b[0])
    h = bytes_ref[...].astype(F32) + mm(spread_matrix(), g_ref[...])
    out = block_forward(h, gains, (wq, wo, wu, wd), wait, 3, a_ref, qkv_ref, p_ref, o_ref, mid_ref, c_ref, u_ref, gp_ref)
    live = live_rows(scal)
    y_ref[...] = jnp.where(live, out, 0.0).astype(BF16)
    dm_ref[...] = jnp.where(live, cot_ref[...].astype(F32), 0.0).astype(BF16)


def row_block(*shape):
    return pl.BlockSpec(shape, lambda i, s: (i,) + (0,) * (len(shape) - 1))


def const_block(*shape):
    return pl.BlockSpec(shape, lambda i, s: (0,) * len(shape), pipeline_mode=pl.Buffered(1))


def seq_block():
    return pl.BlockSpec((TILE, D), lambda i, s: (s[0] * TILES + i, 0))


def local_forward(scal, states, cotangent, g_own, gains, weights, gains_b, weights_b):
    outs = (
        ((SEQ, D), BF16), ((SEQ, D), BF16), ((SEQ, D), BF16), ((SEQ, 3 * D), BF16),
        ((SEQ // 128, PAIRS, 128, 256), BF16), ((SEQ, D), BF16), ((SEQ, D), F32), ((SEQ, D), BF16),
        ((SEQ, FF), BF16), ((SEQ, FF), BF16),
    )
    return pl.pallas_call(
        local_forward_kernel,
        name="local_forward",
        out_shape=[sds(*o) for o in outs],
        grid_spec=pltpu.PrefetchScalarGridSpec(
            num_scalar_prefetch=1,
            grid=(TILES,),
            in_specs=[seq_block(), seq_block(), row_block(TILE // PATCH, D), const_block(1, 2, D)]
            + [ANY] * 8 + [const_block(1, 2, D)],
            out_specs=[row_block(o[0][0] // TILES, *o[0][1:]) for o in outs],
            scratch_shapes=[
                WSCRATCH["q"], WSCRATCH["o"], WSCRATCH["u"], WSCRATCH["d"], pltpu.SemaphoreType.DMA((4,)),
            ],
        ),
        compiler_params=pltpu.CompilerParams(vmem_limit_bytes=VLIMIT),
        cost_estimate=cost(14.5e9, 60e6),
    )(scal, states, cotangent, g_own, gains, *weights, *weights_b, gains_b)


def local_dz_kernel(scal, dm_ref, gp_ref, wd_a, wd_b, dz_ref, wd, wsem):
    wait = start_weights(scal, ((wd_a, wd_b, wd),), wsem, (0,))
    wait(0)
    for part in range(FF // D):
        cols = slice(part * D, part * D + D)
        du = mm_nt(dm_ref[...], wd[cols, :])
        dz_ref[:, cols] = (du * gp_ref[:, cols].astype(F32)).astype(BF16)


def local_dz(scal, dm, gp, wd_a, wd_b):
    return pl.pallas_call(
        local_dz_kernel,
        name="local_dz",
        out_shape=sds((SEQ, FF), BF16),
        grid_spec=pltpu.PrefetchScalarGridSpec(
            num_scalar_prefetch=1,
            grid=(TILES,),
            in_specs=[row_block(TILE, D), row_block(TILE, FF), ANY, ANY],
            out_specs=row_block(TILE, FF),
            scratch_shapes=[WSCRATCH["d"], pltpu.SemaphoreType.DMA((1,))],
        ),
        compiler_params=pltpu.CompilerParams(vmem_limit_bytes=VLIMIT),
        cost_estimate=cost(4.8e9, 18e6),
    )(scal, dm, gp, wd_a, wd_b)


def local_backward_kernel(
    scal, dz_ref, dm_ref, bytes_ref, g_ref, mid_ref, qkv_ref, p_ref, gains_ref,
    wq_a, wo_a, wu_a, wq_b, wo_b, wu_b, gains_b,
    dr_ref, dqkv_ref, dh_ref, dg_ref, dgain_ref,
    do_s, wq, wo, wu, wsem,
):
    pairs = ((wq_a, wq_b, wq), (wo_a, wo_b, wo), (wu_a, wu_b, wu))
    wait = start_weights(scal, pairs, wsem, (2, 1, 0))
    gains = jnp.where(scal[0] == 1, gains_ref[0], gains_b[0])
    h = bytes_ref[...].astype(F32) + mm(spread_matrix(), g_ref[...])
    dh, dgain = block_backward(
        dm_ref[...].astype(F32), h, gains, (wq, wo, wu), wait, dz_ref, mid_ref, qkv_ref, p_ref, do_s, dr_ref, dqkv_ref
    )
    dh_ref[...] = dh
    dg_ref[...] = jnp.sum(dh.reshape(TILE // PATCH, PATCH, D), axis=1).astype(BF16)

    @pl.when(pl.program_id(0) == 0)
    def _():
        dgain_ref[...] = jnp.zeros_like(dgain_ref)

    dgain_ref[0:2, :] += dgain


def local_backward(scal, dz, dm, states, g_own, mid, qkv, p, gains, weights, gains_b, weights_b):
    outs = (
        ((SEQ, D), BF16), ((SEQ, 3 * D), BF16), ((SEQ, D), F32), ((PATCHES, D), BF16), ((8, D), F32),
    )
    return pl.pallas_call(
        local_backward_kernel,
        name="local_backward",
        out_shape=[sds(*o) for o in outs],
        grid_spec=pltpu.PrefetchScalarGridSpec(
            num_scalar_prefetch=1,
            grid=(TILES,),
            in_specs=[
                row_block(TILE, FF), row_block(TILE, D), seq_block(), row_block(TILE // PATCH, D), row_block(TILE, D),
                row_block(TILE, 3 * D), row_block(SUBS, PAIRS, 128, 256), const_block(1, 2, D),
            ] + [ANY] * 6 + [const_block(1, 2, D)],
            out_specs=[row_block(o[0][0] // TILES, *o[0][1:]) for o in outs[:4]] + [const_block(8, D)],
            scratch_shapes=[
                pltpu.VMEM((TILE, D), BF16), WSCRATCH["q"], WSCRATCH["o"], WSCRATCH["u"], pltpu.SemaphoreType.DMA((3,)),
            ],
        ),
        compiler_params=pltpu.CompilerParams(vmem_limit_bytes=VLIMIT),
        cost_estimate=cost(10e9, 50e6),
    )(scal, dz, dm, states, g_own, mid, qkv, p, gains, *weights, *weights_b, gains_b)


def store_shards(scal, total, keep_ref, send_ref, add_refs, order, r, count, z):
    first, second = order
    position = {"x": scal[1], "y": scal[2]}
    for one in range(2):
        for two in range(2):
            at = {first: one ^ position[first], second: two ^ position[second]}
            for k in range(count // 4):
                level = (k ^ scal[3]) * 4 if count == 16 else 0
                shard = level + at["y"] * 2 + at["x"]
                value = total[pl.ds(pl.multiple_of(shard * r, 16), r), :]
                if add_refs is not None:
                    value = value + add_refs[one][two, k].astype(F32)
                (send_ref if one else keep_ref)[two, k] = value.astype(BF16)


def weight_grad_kernel(scal, *refs, parts, order, r, count, has_add, core_zero, shards):
    xs, dys, refs = refs[:parts], refs[parts : 2 * parts], refs[2 * parts :]
    adds = None
    if has_add:
        adds, refs = refs[:2], refs[2:]

    def work():
        value = mm_tn(xs[0][...], dys[0][...])
        for x, dy in zip(xs[1:], dys[1:]):
            value = value + mm_tn(x[...], dy[...])
        if not shards:
            refs[0][...] = value
            return
        keep_ref, send_ref, total = refs
        total[...] = value
        store_shards(scal, total, keep_ref, send_ref, adds, order, r, count, pl.program_id(0))

    if core_zero:
        pl.when(scal[0] == 0)(work)
    else:
        work()


def weight_grad(scal, xs, x_lo, dys, dy_lo, rows, cols, tn, order, add=None, half=None, core_zero=False, shards=True):
    mt, nt = rows // D, cols // tn
    r = rows // 16
    count = 16 if mt == 1 else 4
    depth = xs[0].shape[0]
    kz = 4 if mt == 1 else 1

    def dy_map(m, n, s):
        offset = 0 if half is None else (s[0] if half == "own" else 1 - s[0]) * nt
        return (0, dy_lo // tn + offset + n)

    shard_spec = pl.BlockSpec((2, kz, r, tn), lambda m, n, s: (0, 0 if mt == 1 else m ^ s[3], 0, n))
    if shards:
        out_shape = [sds((2, 4, r, cols), BF16)] * 2
        out_specs = [shard_spec] * 2
        scratch = [pltpu.VMEM((D, tn), F32)]
    else:
        out_shape = sds((rows, cols), F32)
        out_specs = pl.BlockSpec((D, tn), lambda m, n, s: (m, n))
        scratch = []
    return pl.pallas_call(
        functools.partial(
            weight_grad_kernel, parts=len(xs), order=order, r=r, count=count, has_add=add is not None,
            core_zero=core_zero, shards=shards,
        ),
        name="weight_grad",
        out_shape=out_shape,
        grid_spec=pltpu.PrefetchScalarGridSpec(
            num_scalar_prefetch=1,
            grid=(mt, nt),
            in_specs=[pl.BlockSpec((depth, D), lambda m, n, s: (0, x_lo // D + m))] * len(xs)
            + [pl.BlockSpec((depth, tn), dy_map)] * len(xs) + [shard_spec] * (0 if add is None else 2),
            out_specs=out_specs,
            scratch_shapes=scratch,
        ),
        compiler_params=pltpu.CompilerParams(vmem_limit_bytes=VLIMIT),
        cost_estimate=cost(2 * depth * len(xs) * rows * cols, 2 * (depth * (rows + cols) + rows * cols)),
    )(scal, *xs, *dys, *(add or ()))


def patch_grad_kernel(scal, bytes_ref, dpp_ref, *refs, order, shards):
    bytes_f32, total = refs[-2:]

    @pl.when(pl.program_id(0) == 0)
    def _():
        fill_lanes(bytes_f32, bytes_ref)

    byte = scal[0] * (PATCH // 2) + pl.program_id(0)
    x = strided_rows(bytes_f32, byte, MB * PATCHES).astype(BF16)
    value = mm_tn(x, dpp_ref[...])
    if not shards:
        refs[0][...] = value
        return
    total[...] = value
    store_shards(scal, total, refs[0], refs[1], None, order, 192, 4, pl.program_id(0))


def patch_weight_grad(scal, states, dpp, order, shards=True):
    if shards:
        out_shape = [sds((2, 4, 192, D), BF16)] * 2
        out_specs = [pl.BlockSpec((2, 1, 192, D), lambda i, s: (0, i ^ s[3], 0, 0))] * 2
    else:
        out_shape = [sds((PATCH // 2 * D, D), F32)]
        out_specs = [pl.BlockSpec((D, D), lambda i, s: (i, 0))]
    return pl.pallas_call(
        functools.partial(patch_grad_kernel, order=order, shards=shards),
        name="patch_weight_grad",
        out_shape=out_shape,
        grid_spec=pltpu.PrefetchScalarGridSpec(
            num_scalar_prefetch=1,
            grid=(PATCH // 2,),
            in_specs=[const_block(MB * SEQ, D), const_block(MB * PATCHES, D)],
            out_specs=out_specs,
            scratch_shapes=[pltpu.VMEM((LANES, MB * SEQ, 128), F32), pltpu.VMEM((D, D), F32)],
        ),
        compiler_params=pltpu.CompilerParams(vmem_limit_bytes=VLIMIT),
        cost_estimate=cost(1.2e9, 10e6),
    )(scal, states, dpp)


def input_grad_kernel(dpp_ref, dh_ref, wp_hbm, out_ref, acc, wp, psem):
    copies = [
        pltpu.make_async_copy(wp_hbm.at[pl.ds(j * D, D)], wp.at[pl.ds(j * D, D)], psem.at[j]) for j in range(PATCH)
    ]
    for copy in copies:
        copy.start()
    for j in range(PATCH):
        copies[j].wait()
        value = mm_nt(dpp_ref[...], wp[j * D : j * D + D, :])
        for b in range(LANES):
            acc[b, pl.ds(j, PATCHES, stride=PATCH), :] = value[:, b * 128 : b * 128 + 128]
    for b in range(LANES):
        cols = slice(b * 128, b * 128 + 128)
        out_ref[:, cols] = (dh_ref[:, cols] + acc[b]).astype(BF16)


def input_grad_part(dpp_own, dh, patch_weight):
    return pl.pallas_call(
        input_grad_kernel,
        name="input_grad",
        out_shape=sds((SEQ, D), BF16),
        in_specs=[pl.BlockSpec(memory_space=pltpu.VMEM)] * 2 + [ANY],
        out_specs=pl.BlockSpec(memory_space=pltpu.VMEM),
        scratch_shapes=[
            pltpu.VMEM((LANES, SEQ, 128), F32), pltpu.VMEM((PATCH * D, D), BF16), pltpu.SemaphoreType.DMA((PATCH,)),
        ],
        compiler_params=pltpu.CompilerParams(vmem_limit_bytes=VLIMIT),
        cost_estimate=cost(1.2e9, 15e6),
    )(dpp_own, dh, patch_weight)


def swap_core(value):
    return lax.ppermute(value, "section", [(0, 1), (1, 0)])


def hop(value, mask, cores):
    size = lax.axis_size("dp")
    if cores == (0, 1):
        return lax.ppermute(value, "dp", [(i, i ^ mask) for i in range(size)])
    pairs = [(c * size + i, c * size + (i ^ mask)) for c in cores for i in range(size)]
    return lax.ppermute(value, ("section", "dp"), pairs)


HOPS = {"x": 1, "y": 2}


def add_low(a, b):
    return (a.astype(F32) + b.astype(F32)).astype(BF16)


def z_sum(keep, recv, cores):
    total = keep[..., 0, :, :].astype(F32) + recv[..., 0, :, :].astype(F32)
    for k in (1, 2, 3):
        part = hop(add_low(keep[..., k, :, :], recv[..., k, :, :]), 4 * k, cores)
        total = total + part.astype(F32)
    return total


def reduce_shards(keep, send, order, cores=(0, 1)):
    recv = hop(send, HOPS[order[0]], cores)
    kept, sent = add_low(keep[0], recv[0]), add_low(keep[1], recv[1])
    return z_sum(kept, hop(sent, HOPS[order[1]], cores), cores)


def local_weight_grads(scal, x, dy, rows, cols, tn, order):
    half = cols // 2
    peer = weight_grad(scal, [x], 0, [dy], 0, rows, half, tn, order, half="peer")
    return weight_grad(
        scal, [x], 0, [dy], 0, rows, half, tn, order, add=[swap_core(v) for v in peer], half="own"
    )


def body(states, lengths, patch_weight, w_qkv, w_out, w_up, w_down, gains, cotangent):
    size = lax.axis_size("dp")
    fast = size == 16
    core = lax.axis_index("section")
    at = lax.axis_index("dp")
    mx, my, mz = at % 2, (at // 2) % 2, (at // 4) % 4
    length = jnp.where(core == 0, lengths[0], lengths[1])
    scal = jnp.stack([core, mx, my, mz, length]).astype(jnp.int32)
    weights = (w_qkv, w_out, w_up, w_down)
    other = tuple(swap_core(w) for w in weights)
    gains_other = swap_core(gains)

    g_all, xg, start, qkv_g, p_g, mid_g, gp_g = global_forward(scal, states, gains, patch_weight, weights)
    g_recv = swap_core(g_all[PATCHES:])
    g_own = jnp.where(core == 0, g_all[:PATCHES], g_recv)
    if fast:
        xg_next = hop(xg, 1, (0,))

    y, dm, a, qkv, p, o, mid, c, u, gp = local_forward(
        scal, states, cotangent, g_own, gains, weights, gains_other, other
    )
    y_recv = swap_core(y)
    g_rows = jnp.broadcast_to(g_all[:, None, :], (MB * PATCHES, PATCH, D)).reshape(MB * SEQ, D)
    section_outputs = jnp.where(core == 0, g_rows, jnp.concatenate([y_recv, y], axis=0))[None]

    if fast:
        down_l = reduce_shards(*local_weight_grads(scal, u, dm, FF, D, 384, "xy"), "xy")
    dz = local_dz(scal, dm, gp, w_down, other[3])
    if fast:
        up_l = reduce_shards(*local_weight_grads(scal, c, dz, D, FF, 384, "yx"), "yx")
    dr, dqkv, dh, dg, dgain_l = local_backward(
        scal, dz, dm, states, g_own, mid, qkv, p, gains, weights[:3], gains_other, other[:3]
    )
    dg_recv = swap_core(dg)
    dpp, dy_keep, dy_send, dgain_g = global_backward(
        scal, (dg, dg_recv), (start, mid_g, qkv_g, p_g, gp_g), gains, weights
    )
    dpp_recv = swap_core(dpp)
    dpp = jnp.where(core == 0, dpp, dpp_recv)
    dpp_own = jnp.where(core == 0, dpp[:PATCHES], dpp[PATCHES:])
    own_grad = input_grad_part(dpp_own, dh, patch_weight)
    peer_grad = swap_core(own_grad)
    input_grad = jnp.where(
        core == 0, jnp.concatenate([own_grad, peer_grad]), jnp.concatenate([peer_grad, own_grad])
    ).astype(F32)

    blocks = jnp.stack([jnp.where(core == 0, dgain_g[:2], 0.0), dgain_l[:2]])
    blocks = lax.psum(blocks, ("section", "dp"))
    own_gains = jnp.where(core == 0, blocks[0], blocks[1])
    share = D // size
    gain_grad = lax.dynamic_slice(own_gains, (0, at * share), (2, share))

    if fast:
        proj_l = reduce_shards(*local_weight_grads(scal, o, dr, D, D, 384, "xy"), "xy")
        qkv_l = reduce_shards(*local_weight_grads(scal, a, dqkv, D, 3 * D, 384, "xy"), "xy")
        dy_next = hop(dy_send, 1, (0,))
        keep, send = patch_weight_grad(scal, states, dpp, "yx")
        patch_grad = reduce_shards(keep, send, "yx")

        def global_grad(x_lo, dy_lo, rows, cols):
            keep, send = weight_grad(
                scal, [xg, xg_next], x_lo, [dy_keep, dy_next], dy_lo, rows, cols, 384, "yx", core_zero=True
            )
            both = z_sum(keep, hop(send, 2, (0,)), (0,))
            swapped = hop(both[1].astype(BF16), 1, (0,)).astype(F32)
            mine = both[0]
            return jnp.where(
                mx == 0, jnp.concatenate([mine, swapped], axis=1), jnp.concatenate([swapped, mine], axis=1)
            )

        half = D // 2
        up_g = global_grad(2 * D, 4 * half, D, FF // 2)
        down_g = global_grad(3 * D, 8 * half, FF, half)
        proj_g = global_grad(D, 3 * half, D, half)
        qkv_g = global_grad(0, 0, D, 3 * half)

        def place(whole, part):
            other_part = swap_core(part)
            return jnp.where(core == 0, whole, jnp.concatenate([other_part, part], axis=1))[None]

        outs = (place(qkv_g, qkv_l), place(proj_g, proj_l), place(up_g, up_l), place(down_g, down_l))
    else:
        (patch_half,) = patch_weight_grad(scal, states, dpp, "xy", shards=False)
        patch_grad = lax.psum_scatter(patch_half, "dp", scatter_dimension=0, tiled=True)
        half = D // 2
        swap_halves = lambda keep, send, lo, width: jnp.where(
            mx == 0,
            jnp.concatenate([keep[:, lo : lo + width], send[:, lo : lo + width]], axis=1),
            jnp.concatenate([send[:, lo : lo + width], keep[:, lo : lo + width]], axis=1),
        )

        def whole_grad(x_lo, dy_lo, x, dy, rows, cols):
            dy_g = swap_halves(dy_keep, dy_send, dy_lo, cols // 2)
            glob = weight_grad(scal, [xg], x_lo, [dy_g], 0, rows, cols, 384, "xy", shards=False)
            loc = weight_grad(scal, [x], 0, [dy], 0, rows, cols, 384, "xy", shards=False)
            total = jnp.where(core == 0, glob, loc + swap_core(loc))
            return lax.psum_scatter(total, "dp", scatter_dimension=0, tiled=True)[None]

        outs = (
            whole_grad(0, 0, a, dqkv, D, 3 * D),
            whole_grad(D, 3 * half, o, dr, D, D),
            whole_grad(2 * D, 4 * half, c, dz, D, FF),
            whole_grad(3 * D, 8 * half, u, dm, FF, D),
        )
    return (section_outputs, input_grad, patch_grad, *outs, gain_grad[None])


def solution(mesh):
    return jax.shard_map(
        body,
        mesh=mesh,
        in_specs=(
            P("dp", None), P("dp"), P(), P("section", None, None), P("section", None, None),
            P("section", None, None), P("section", None, None), P("section", None, None), P("dp", None),
        ),
        out_specs=(
            P("section", "dp", None), P("dp", None), P(("section", "dp"), None), P("section", "dp", None),
            P("section", "dp", None), P("section", "dp", None), P("section", "dp", None), P("section", None, "dp"),
        ),
        check_vma=False,
    )
```

time: 1780 us -> 578 us (0.32)
  waiting for transfers between devices: 917 us -> 134 us
  starting transfers between devices: 472 us -> 113 us
  Pallas kernels: 0 us -> 236 us
  matrix products: 153 us -> 0 us
  local copies, waits for them, and re-layouts: 110 us -> 15.2 us
  other arithmetic: 80.9 us -> 25.2 us
  blocking collectives: 0 us -> 41.1 us
  loops' own time: 18.9 us -> 0 us
    reduce_scatter x5 -> x0, waiting for transfers between devices: 846 us -> none  [the longest x1 212 us: body(): lax.psum_scatter(patch_total, ('section', 'dp'), scatter_dimension=0, til...]
    ppermute x3 -> x69, starting transfers between devices: 471 us -> 113 us  [the longest x22 72.2 us: hop(): return lax.ppermute(value, ('section', 'dp'), pairs)]
    pallas_call x0 -> x19, Pallas kernels: none -> 236 us  [the longest x12 77 us: weight_grad(): pl.pallas_call(functools.partial(weight_grad_kernel, parts=len(xs), order...]
    dot_general x50 -> x0, matrix products: 151 us -> none  [the longest x10 55.9 us: product_tn(): lax.dot_general(left, right, (((0,), (0,)), ((), ())), preferred_element_...]
    ppermute x3 -> x69, waiting for transfers between devices: 2.72 us -> 134 us  [the longest x22 101 us: hop(): return lax.ppermute(value, ('section', 'dp'), pairs)]
    unnamed x8 -> x0, waiting for transfers between devices: 67.6 us -> none
    add x9, other arithmetic: 58.4 us -> 2.71 us  [z_sum(): total = total + part.astype(F32)]
    psum x0 -> x1, blocking collectives: none -> 41.1 us  [body(): blocks = lax.psum(blocks, ('section', 'dp'))]
  transfers between devices with their start and end apart: 10 -> 69, of which waited for: 8 -> 24; matrix products, arithmetic and copies ran while one was open for 4% -> 6% of each run, Pallas kernels for 0% -> 24%
where the time goes in v1:
time: 578 us; the launch traced here: 567 us
  Pallas kernels  236 us (41%)
  waiting for transfers between devices  134 us (23%)
  starting transfers between devices  113 us (20%)
  blocking collectives  41.1 us (7%)
  other arithmetic  25.2 us (4%)
  local copies, waits for them, and re-layouts  15.2 us (3%)
    ppermute x22, waiting for transfers between devices, hop(): return lax.ppermute(value, ('section', 'dp'), pairs)  101 us
    pallas_call x12, Pallas kernels, weight_grad(): pl.pallas_call(functools.partial(weight_grad_kernel, parts=len(xs), order...  77 us
    ppermute x22, starting transfers between devices, hop(): return lax.ppermute(value, ('section', 'dp'), pairs)  72.2 us
    pallas_call x1, Pallas kernels, local_forward(): pl.pallas_call(local_forward_kernel, name='local_forward', out_shape=[sds...  45 us
    pallas_call x1, Pallas kernels, local_backward(): pl.pallas_call(local_backward_kernel, name='local_backward', out_shape=[s...  43.4 us
    psum x1, blocking collectives, body(): blocks = lax.psum(blocks, ('section', 'dp'))  41.1 us
    ppermute x25, starting transfers between devices, hop(): return lax.ppermute(value, 'dp', [(i, i ^ mask) for i in range(size)])  35.7 us
    ppermute x25, waiting for transfers between devices, hop(): return lax.ppermute(value, 'dp', [(i, i ^ mask) for i in range(size)])  31 us
  transfers between devices with their start and end apart: 69, of which 24 were waited for; matrix products, arithmetic and copies ran while one was open for 6% of the time, Pallas kernels for 24%

profile of v1, /device:TPU:8, one launch (start us, length us, event | category | flops | bytes accessed | tf_op | source)
XLA Modules:
  0.0 567.1 jit_solution(11478202256901700882)
XLA Ops:
  5.0 23.6 %global_forward.1 = (bf16[256,768]{1,0:T(8,128)(2,1)}, bf16[256,5376]{1,0:T(8,128)(2,1)}, f32[256,768]{1,0:T(8,128)}, bf16[256,2304]{1,0:T(8,128)(2,1)}, bf16[2,...) custom-call(s32[5]{0:T(128)} %stack.32.scal, bf16[2048,768]{1,0:T(8,128)(2,1)} %bytes_ref.7, ...), custom_call_target="tpu_custom_call" | custom-call | flops 6000000000 | bytes 32000000 | tf_op jit(solution)/shard_map/global_forward/pallas_call | solution.py:246
  35.6 45.0 %local_forward.1 = (bf16[1024,768]{1,0:T(8,128)(2,1)}, bf16[1024,768]{1,0:T(8,128)(2,1)}, bf16[1024,768]{1,0:T(8,128)(2,1)}, bf16[1024,2304]{1,0:T(8,128)(2,1)},...) custom-call(s32[5]{0:T(128)} %stack.32.scal, ...), custom_call_target="tpu_custom_call" | custom-call | flops 14499999744 | bytes 60000000 | tf_op jit(solution)/shard_map/local_forward/pallas_call | solution.py:396
  80.6 12.4 %local_dz.1.dz_ref.refs_1_ = bf16[1024,3072]{1,0:T(8,128)(2,1)} custom-call(s32[5]{0:T(128)} %stack.32.scal, bf16[1024,768]{1,0:T(8,128)(2,1)} %get-tuple-element.62.dm_ref.refs_1_, bf16[1024,3072]{1,0:T(8,128)(2,1)} %get-tuple-element.63.gp_ref, bf16[1,3072,768]{2,1,0:T(8,128)(2,1)} %wd_hbm.3, bf16[1,3072,768]{2,1,0:T(8,128)(2,1)} %collective-permute-done.4.wd_b), custom_call_target="tpu_custom_call" | custom-call | flops 4800000000 | bytes 18000000 | tf_op jit(solution)/shard_map/local_dz/pallas_call | solution.py:425
  93.0 43.4 %local_backward.1 = (bf16[1024,768]{1,0:T(8,128)(2,1)}, bf16[1024,2304]{1,0:T(8,128)(2,1)}, f32[1024,768]{1,0:T(8,128)}, bf16[128,768]{1,0:T(8,128)(2,1)}, f32[8,768]{1,0:T(8,128)}) custom-call(s32[5]{0:T(128)} %stack.32.scal, bf16[1024,3072]{1,0:T(8,128)(2,1)} %local_dz.1.dz_ref.refs_1_, bf16[1024,768]{1,0:T(8,128)(2,1)} %get-tuple-element.62.dm_ref.refs_1_, ...), custom_call_target="tpu_custom_call" | custom-call | flops 10000000000 | bytes 50000000 | tf_op jit(solution)/shard_map/local_backward/pallas_call | solution.py:468
  136.9 4.1 weight_grad.16
  141.5 8.2 %weight_grad.22 = (bf16[2,4,192,384]{3,2,1,0:T(8,128)(2,1)}, bf16[2,4,192,384]{3,2,1,0:T(8,128)(2,1)}) custom-call(s32[5]{0:T(128)} %stack.32.scal, bf16[1024,3072]{1,0:T(8,128)(2,1)} %get-tuple-element.105.refs_0_, bf16[1024,768]{1,0:T(8,128)(2,1)} %get-tuple-element.62.dm_ref.refs_1_), custom_call_target="tpu_custom_call" | custom-call | flops 2415919104 | bytes 9437184 | tf_op jit(solution)/shard_map/weight_grad/pallas_call | solution.py:547
  149.7 6.7 %weight_grad.13 = (bf16[2,4,48,1152]{3,2,1,0:T(8,128)(2,1)}, bf16[2,4,48,1152]{3,2,1,0:T(8,128)(2,1)}) custom-call(s32[5]{0:T(128)} %stack.32.scal, bf16[1024,768]{1,0:T(8,128)(2,1)} %get-tuple-element.82.refs_0_, bf16[1024,2304]{1,0:T(8,128)(2,1)} %get-tuple-element.83.refs_1_), custom_call_target="tpu_custom_call" | custom-call | flops 1811939328 | bytes 5701632 | tf_op jit(solution)/shard_map/weight_grad/pallas_call | solution.py:547
  158.3 4.3 weight_grad.17
  164.7 17.6 %global_backward.1 = (bf16[256,768]{1,0:T(8,128)(2,1)}, bf16[256,3456]{1,0:T(8,128)(2,1)}, bf16[256,3456]{1,0:T(8,128)(2,1)}, f32[8,768]{1,0:T(8,128)}) custom-call(s32[5]{0:T(128)} %stack.32.scal, bf16[128,768]{1,0:T(8,128)(2,1)} %get-tuple-element.67.dg0_ref, bf16[128,768]{1,0:T(8,128)(2,1)} %copy-done.27, f32[256,768]{1,0:T(8,128)} %get-tuple-element.68.start_ref, ...), custom_call_target="tpu_custom_call" | custom-call | flops 6000000000 | bytes 24000000 | tf_op jit(solution)/shard_map/global_backward/pallas_call | solution.py:315
  184.1 8.1 %weight_grad.19 = (bf16[2,4,48,1536]{3,2,1,0:T(8,128)(2,1)}, bf16[2,4,48,1536]{3,2,1,0:T(8,128)(2,1)}) custom-call(s32[5]{0:T(128)} %stack.32.scal, bf16[1024,768]{1,0:T(8,128)(2,1)} %get-tuple-element.98.refs_0_, bf16[1024,3072]{1,0:T(8,128)(2,1)} %local_dz.1.dz_ref.refs_1_), custom_call_target="tpu_custom_call" | custom-call | flops 2415919104 | bytes 7077888 | tf_op jit(solution)/shard_map/weight_grad/pallas_call | solution.py:547
  192.9 2.6 collective-permute-start.40
  197.9 2.5 collective-permute-start.41
  203.0 41.1 %psum.7 = f32[2,2,768]{2,1,0:T(2,128)S(1)} all-reduce(f32[2,2,768]{2,1,0:T(2,128)S(1)} %pad_maximum_fusion), channel_id=1, replica_groups=mesh['section'=2,'dp'=16] {'section','dp'}, use_global_device_ids=true, to_apply=%region_0.1 | all-reduce | flops 3072 | bytes 24576 | tf_op jit(solution)/shard_map/psum | solution.py:726
  244.1 4.2 collective-permute-start.15
  251.3 7.2 %weight_grad.14 = (bf16[2,4,48,1152]{3,2,1,0:T(8,128)(2,1)}, bf16[2,4,48,1152]{3,2,1,0:T(8,128)(2,1)}) custom-call(s32[5]{0:T(128)} %stack.32.scal, bf16[1024,768]{1,0:T(8,128)(2,1)} %get-tuple-element.82.refs_0_, bf16[1024,2304]{1,0:T(8,128)(2,1)} %get-tuple-element.83.refs_1_, bf16[2,4,48,1152]{3,2,1,0:T(8,128)(2,1)} %collective-permute-done.22.refs_2_, ...), custom_call_target="tpu_custom_call" | custom-call | flops 1811939328 | bytes 5701632 | tf_op jit(solution)/shard_map/weight_grad/pallas_call | solution.py:547
  258.6 7.5 %patch_weight_grad.1 = (bf16[2,4,192,768]{3,2,1,0:T(8,128)(2,1)}, bf16[2,4,192,768]{3,2,1,0:T(8,128)(2,1)}) custom-call(s32[5]{0:T(128)} %stack.32.scal, bf16[2048,768]{1,0:T(8,128)(2,1)} %bytes_ref.7, bf16[256,768]{1,0:T(8,128)(2,1)} %copy-done.7), custom_call_target="tpu_custom_call" | custom-call | flops 1200000000 | bytes 10000000 | tf_op jit(solution)/shard_map/patch_weight_grad/pallas_call | solution.py:591
  266.0 4.3 collective-permute-start.16
  270.4 9.7 %input_grad.1 = bf16[1024,768]{1,0:T(8,128)(2,1)} custom-call(bf16[128,768]{1,0:T(8,128)(2,1)} %slice_select_fusion.dpp_ref, f32[1024,768]{1,0:T(8,128)} %get-tuple-element.74.dh_ref, bf16[6144,768]{1,0:T(8,128)(2,1)} %wp_hbm.3), custom_call_target="tpu_custom_call" | custom-call | flops 1200000000 | bytes 15000000 | tf_op jit(solution)/shard_map/input_grad/pallas_call | solution.py:624
  280.1 8.8 %weight_grad.23 = (bf16[2,4,192,384]{3,2,1,0:T(8,128)(2,1)}, bf16[2,4,192,384]{3,2,1,0:T(8,128)(2,1)}) custom-call(s32[5]{0:T(128)} %stack.32.scal, bf16[1024,3072]{1,0:T(8,128)(2,1)} %get-tuple-element.105.refs_0_, bf16[1024,768]{1,0:T(8,128)(2,1)} %get-tuple-element.62.dm_ref.refs_1_, bf16[2,4,192,384]{3,2,1,0:T(8,128)(2,1)} %collective-permute-done.61.refs_2_, ...), custom_call_target="tpu_custom_call" | custom-call | flops 2415919104 | bytes 9437184 | tf_op jit(solution)/shard_map/weight_grad/pallas_call | solution.py:547
  288.9 8.4 %weight_grad.20 = (bf16[2,4,48,1536]{3,2,1,0:T(8,128)(2,1)}, bf16[2,4,48,1536]{3,2,1,0:T(8,128)(2,1)}) custom-call(s32[5]{0:T(128)} %stack.32.scal, bf16[1024,768]{1,0:T(8,128)(2,1)} %get-tuple-element.98.refs_0_, bf16[1024,3072]{1,0:T(8,128)(2,1)} %local_dz.1.dz_ref.refs_1_, bf16[2,4,48,1536]{3,2,1,0:T(8,128)(2,1)} %collective-permute-done.48.refs_2_, ...), custom_call_target="tpu_custom_call" | custom-call | flops 2415919104 | bytes 7077888 | tf_op jit(solution)/shard_map/weight_grad/pallas_call | solution.py:547
  298.4 2.1 collective-permute-start.50
  300.4 2.4 add_convert_fusion.7
  302.9 3.5 maximum_select_fusion
  306.3 10.9 %collective-permute-done.16.refs_3_ = bf16[256,3456]{1,0:T(8,128)(2,1)S(1)} collective-permute-done((bf16[256,3456]{1,0:T(8,128)(2,1)}, bf16[256,3456]{1,0:T(8,128)(2,1)S(1)}, u32[]{:S(2)}, u32[]{:S(2)}) %collective-permute-start.16) | collective-permute-done | bytes 1769504 | tf_op jit(solution)/shard_map/ppermute | solution.py:647
  318.5 6.2 %weight_grad.21 = (bf16[2,4,192,384]{3,2,1,0:T(8,128)(2,1)}, bf16[2,4,192,384]{3,2,1,0:T(8,128)(2,1)}) custom-call(s32[5]{0:T(128)} %stack.32.scal, bf16[256,5376]{1,0:T(8,128)(2,1)} %get-tuple-element.77.refs_0_, bf16[256,5376]{1,0:T(8,128)(2,1)} %copy-done.1, bf16[256,3456]{1,0:T(8,128)(2,1)} %get-tuple-element.78.refs_2_, bf16[256,3456]{1,0:T(8,128)(2,1)} %copy-done.2), custom_call_target="tpu_custom_call" | custom-call | flops 1207959552 | bytes 4128768 | tf_op jit(solution)/shard_map/weight_grad/pallas_call | solution.py:547
  326.1 6.3 %weight_grad.18 = (bf16[2,4,48,1536]{3,2,1,0:T(8,128)(2,1)}, bf16[2,4,48,1536]{3,2,1,0:T(8,128)(2,1)}) custom-call(s32[5]{0:T(128)} %stack.32.scal, bf16[256,5376]{1,0:T(8,128)(2,1)} %get-tuple-element.77.refs_0_, bf16[256,5376]{1,0:T(8,128)(2,1)} %copy-done.1, bf16[256,3456]{1,0:T(8,128)(2,1)} %get-tuple-element.78.refs_2_, bf16[256,3456]{1,0:T(8,128)(2,1)} %copy-done.2), custom_call_target="tpu_custom_call" | custom-call | flops 1207959552 | bytes 3538944 | tf_op jit(solution)/shard_map/weight_grad/pallas_call | solution.py:547
  333.7 3.4 weight_grad.15
  338.1 4.0 collective-permute-start.30
  342.1 5.5 weight_grad.12
  350.1 2.8 collective-permute-start.27
  353.7 3.1 collective-permute-start.31
  356.9 4.4 fusion
  363.3 3.8 collective-permute-start.32
  367.1 2.5 collective-permute-start.33
  370.7 2.6 collective-permute-done.33
  373.4 2.5 collective-permute-start.56
  376.0 3.3 collective-permute-start.17
  383.4 3.4 collective-permute-done.34
  386.9 3.0 collective-permute-start.43
  391.6 34.2 %collective-permute-done.17 = bf16[2,4,48,1152]{3,2,0,1:T(8,128)(2,1)S(1)} collective-permute-done((bf16[2,4,48,1152]{3,2,0,1:T(8,128)(2,1)S(1)}, bf16[2,4,48,1152]{3,2,0,1:T(8,128)(2,1)S(1)}, u32[]{:S(2)}, u32[]{:S(2)}) %collective-permute-start.17) | collective-permute-done | bytes 884768 | tf_op jit(solution)/shard_map/ppermute | solution.py:647
  430.4 5.2 collective-permute-done.51
  435.6 3.1 collective-permute-start.19
  438.9 5.9 %collective-permute-done.64 = bf16[4,192,384]{2,1,0:T(8,128)(2,1)S(1)} collective-permute-done((bf16[4,192,384]{2,1,0:T(8,128)(2,1)S(1)}, bf16[4,192,384]{2,1,0:T(8,128)(2,1)S(1)}, u32[]{:S(2)}, u32[]{:S(2)}) %collective-permute-start.64) | collective-permute-done | bytes 589856 | tf_op jit(solution)/shard_map/ppermute | solution.py:645
  444.7 3.5 collective-permute-start.20
  450.5 4.4 collective-permute-done.20
  457.5 2.9 collective-permute-start.53
  464.1 3.9 collective-permute-start.11
  468.5 4.6 collective-permute-start.21
  473.6 2.1 collective-permute-start.44
  475.9 16.9 %collective-permute-done.21 = bf16[48,1152]{1,0:T(8,128)(2,1)S(1)} collective-permute-done((bf16[48,1152]{1,0:T(8,128)(2,1)S(1)}, bf16[48,1152]{1,0:T(8,128)(2,1)S(1)}, u32[]{:S(2)}, u32[]{:S(2)}) %collective-permute-start.21) | collective-permute-done | bytes 110624 | tf_op jit(solution)/shard_map/ppermute | solution.py:647
  492.8 3.4 collective-permute-start.45
  496.3 3.1 collective-permute-start.46
  500.2 3.5 collective-permute-start.57
  503.8 3.0 collective-permute-done.45
  506.8 5.3 collective-permute-start.58
  512.2 3.1 collective-permute-start.59
  515.6 7.1 %collective-permute-done.58 = bf16[2,192,384]{2,1,0:T(8,128)(2,1)S(1)} collective-permute-done((bf16[2,192,384]{2,1,0:T(8,128)(2,1)S(1)}, bf16[2,192,384]{2,1,0:T(8,128)(2,1)S(1)}, u32[]{:S(2)}, u32[]{:S(2)}) %collective-permute-start.58) | collective-permute-done | bytes 294944 | tf_op jit(solution)/shard_map/ppermute | solution.py:647
  522.7 13.5 %collective-permute-done.59 = bf16[2,192,384]{2,1,0:T(8,128)(2,1)S(1)} collective-permute-done((bf16[2,192,384]{2,1,0:T(8,128)(2,1)S(1)}, bf16[2,192,384]{2,1,0:T(8,128)(2,1)S(1)}, u32[]{:S(2)}, u32[]{:S(2)}) %collective-permute-start.59) | collective-permute-done | bytes 294944 | tf_op jit(solution)/shard_map/ppermute | solution.py:647
  536.5 3.4 collective-permute-start.47
  539.9 2.4 collective-permute-start.60
  543.5 3.4 collective-permute-done.60
  552.6 2.3 collective-permute-done.12
  554.9 5.8 %collective-permute-done.13 = bf16[192,768]{1,0:T(8,128)(2,1)S(1)} collective-permute-done((bf16[192,768]{1,0:T(8,128)(2,1)S(1)}, bf16[192,768]{1,0:T(8,128)(2,1)S(1)}, u32[]{:S(2)}, u32[]{:S(2)}) %collective-permute-start.13) | collective-permute-done | bytes 294944 | tf_op jit(solution)/shard_map/ppermute | solution.py:645
  560.7 5.1 collective-permute-done.14
  (209 shorter events, 67.5 us)
Async XLA Ops:
  0.6 33.2 %collective-permute-start.3 = (bf16[1,768,3072]{2,1,0:T(8,128)(2,1)}, bf16[1,768,3072]{2,1,0:T(8,128)(2,1)}, u32[]{:S(2)}, u32[]{:S(2)}) collective-permute-start(bf16[1,768,3072]{2,1,0:T(8,128)(2,1)} %wu_hbm.3), channel_id=1, source_target_pairs={{0,16},{16,0},{1,17},{17,1},{2,18},{18,2},{3,19},{19,3},{4,20},{20... | collective-permute-start | bytes 14155784 | tf_op jit(solution)/shard_map/ppermute | solution.py:639
  0.7 33.1 %collective-permute-start.4 = (bf16[1,3072,768]{2,1,0:T(8,128)(2,1)}, bf16[1,3072,768]{2,1,0:T(8,128)(2,1)}, u32[]{:S(2)}, u32[]{:S(2)}) collective-permute-start(bf16[1,3072,768]{2,1,0:T(8,128)(2,1)} %wd_hbm.3), channel_id=1, source_target_pairs={{0,16},{16,0},{1,17},{17,1},{2,18},{18,2},{3,19},{19,3},{4,20},{20... | collective-permute-start | bytes 14155784 | tf_op jit(solution)/shard_map/ppermute | solution.py:639
  1.2 32.6 %collective-permute-start.1 = (bf16[1,768,2304]{2,1,0:T(8,128)(2,1)}, bf16[1,768,2304]{2,1,0:T(8,128)(2,1)S(1)}, u32[]{:S(2)}, u32[]{:S(2)}) collective-permute-start(bf16[1,768,2304]{2,1,0:T(8,128)(2,1)} %wq_hbm.3), channel_id=1, source_target_pairs={{0,16},{16,0},{1,17},{17,1},{2,18},{18,2},{3,19},{19,3},{4,20},{20... | collective-permute-start | bytes 10616840 | tf_op jit(solution)/shard_map/ppermute | solution.py:639
  1.3 32.5 %collective-permute-start.2 = (bf16[1,768,768]{2,1,0:T(8,128)(2,1)}, bf16[1,768,768]{2,1,0:T(8,128)(2,1)}, u32[]{:S(2)}, u32[]{:S(2)}) collective-permute-start(bf16[1,768,768]{2,1,0:T(8,128)(2,1)} %wo_hbm.3), channel_id=1, source_target_pairs={{0,16},{16,0},{1,17},{17,1},{2,18},{18,2},{3,19},{19,3},{4,20},{20... | collective-permute-start | bytes 3538952 | tf_op jit(solution)/shard_map/ppermute | solution.py:639
  136.3 27.7 %collective-permute-start.7 = (bf16[128,768]{1,0:T(8,128)(2,1)}, bf16[128,768]{1,0:T(8,128)(2,1)S(1)}, u32[]{:S(2)}, u32[]{:S(2)}) collective-permute-start(bf16[128,768]{1,0:T(8,128)(2,1)} %get-tuple-element.67.dg0_ref), channel_id=1, source_target_pairs={{0,16},{16,0},{1,17},{17,1},{2,18},{18,2},{3,19},{19,3},{4,20},{20... | collective-permute-start | bytes 589832 | tf_op jit(solution)/shard_map/ppermute | solution.py:639
  141.0 15.8 %collective-permute-start.35 = (bf16[2,4,48,384]{3,2,1,0:T(8,128)(2,1)}, bf16[2,4,48,384]{3,2,1,0:T(8,128)(2,1)S(1)}, u32[]{:S(2)}, u32[]{:S(2)}) collective-permute-start(bf16[2,4,48,384]{3,2,1,0:T(8,128)(2,1)} %get-tuple-element.92), channel_id=1, source_target_pairs={{0,16},{16,0},{1,17},{17,1},{2,18},{18,2},{3,19},{19,3},{4,20},{20... | collective-permute-start | bytes 884744 | tf_op jit(solution)/shard_map/ppermute | solution.py:639
  141.0 15.8 %collective-permute-start.36 = (bf16[2,4,48,384]{3,2,1,0:T(8,128)(2,1)}, bf16[2,4,48,384]{3,2,1,0:T(8,128)(2,1)S(1)}, u32[]{:S(2)}, u32[]{:S(2)}) collective-permute-start(bf16[2,4,48,384]{3,2,1,0:T(8,128)(2,1)} %get-tuple-element.93), channel_id=1, source_target_pairs={{0,16},{16,0},{1,17},{17,1},{2,18},{18,2},{3,19},{19,3},{4,20},{20... | collective-permute-start | bytes 884744 | tf_op jit(solution)/shard_map/ppermute | solution.py:639
  149.7 100.2 %collective-permute-start.61 = (bf16[2,4,192,384]{3,2,1,0:T(8,128)(2,1)}, bf16[2,4,192,384]{3,2,1,0:T(8,128)(2,1)}, u32[]{:S(2)}, u32[]{:S(2)}) collective-permute-start(bf16[2,4,192,384]{3,2,1,0:T(8,128)(2,1)} %get-tuple-element.106), channel_id=1, source_target_pairs={{0,16},{16,0},{1,17},{17,1},{2,18},{18,2},{3,19},{19,3},{4,20},{20... | collective-permute-start | bytes 3538952 | tf_op jit(solution)/shard_map/ppermute | solution.py:639
  156.4 87.8 %collective-permute-start.22 = (bf16[2,4,48,1152]{3,2,1,0:T(8,128)(2,1)}, bf16[2,4,48,1152]{3,2,1,0:T(8,128)(2,1)}, u32[]{:S(2)}, u32[]{:S(2)}) collective-permute-start(bf16[2,4,48,1152]{3,2,1,0:T(8,128)(2,1)} %get-tuple-element.84), channel_id=1, source_target_pairs={{0,16},{16,0},{1,17},{17,1},{2,18},{18,2},{3,19},{19,3},{4,20},{20... | collective-permute-start | bytes 2654216 | tf_op jit(solution)/shard_map/ppermute | solution.py:639
  162.6 19.8 %collective-permute-start.37 = (bf16[2,4,48,384]{3,2,1,0:T(8,128)(2,1)}, bf16[2,4,48,384]{3,2,1,0:T(8,128)(2,1)S(1)}, u32[]{:S(2)}, u32[]{:S(2)}) collective-permute-start(bf16[2,4,48,384]{3,2,1,0:T(8,128)(2,1)} %get-tuple-element.95), channel_id=1, source_target_pairs={{0,1},{1,0},{2,3},{3,2},{4,5},{5,4},{6,7},{7,6},{8,9},{9,8},{10,11... | collective-permute-start | bytes 884744 | tf_op jit(solution)/shard_map/ppermute | solution.py:645
  182.3 10.6 %collective-permute-start.8 = (bf16[256,768]{1,0:T(8,128)(2,1)}, bf16[256,768]{1,0:T(8,128)(2,1)}, u32[]{:S(2)}, u32[]{:S(2)}) collective-permute-start(bf16[256,768]{1,0:T(8,128)(2,1)} %get-tuple-element.73), channel_id=1, source_target_pairs={{0,16},{16,0},{1,17},{17,1},{2,18},{18,2},{3,19},{19,3},{4,20},{20... | collective-permute-start | bytes 1179656 | tf_op jit(solution)/shard_map/ppermute | solution.py:639
  182.5 9.9 %collective-permute-start.38 = (bf16[4,48,384]{2,1,0:T(8,128)(2,1)S(1)}, bf16[4,48,384]{2,1,0:T(8,128)(2,1)S(1)}, u32[]{:S(2)}, u32[]{:S(2)}) collective-permute-start(bf16[4,48,384]{2,1,0:T(8,128)(2,1)S(1)} %get-tuple-element.142), channel_id=1, source_target_pairs={{0,2},{1,3},{2,0},{3,1},{4,6},{5,7},{6,4},{7,5},{8,10},{9,11},{10,... | collective-permute-start | bytes 442376 | tf_op jit(solution)/shard_map/ppermute | solution.py:645
  192.2 56.8 %collective-permute-start.23 = (bf16[2,4,48,1152]{3,2,1,0:T(8,128)(2,1)}, bf16[2,4,48,1152]{3,2,1,0:T(8,128)(2,1)}, u32[]{:S(2)}, u32[]{:S(2)}) collective-permute-start(bf16[2,4,48,1152]{3,2,1,0:T(8,128)(2,1)} %get-tuple-element.85), channel_id=1, source_target_pairs={{0,16},{16,0},{1,17},{17,1},{2,18},{18,2},{3,19},{19,3},{4,20},{20... | collective-permute-start | bytes 2654216 | tf_op jit(solution)/shard_map/ppermute | solution.py:639
  196.4 62.1 %collective-permute-start.62 = (bf16[2,4,192,384]{3,2,1,0:T(8,128)(2,1)}, bf16[2,4,192,384]{3,2,1,0:T(8,128)(2,1)}, u32[]{:S(2)}, u32[]{:S(2)}) collective-permute-start(bf16[2,4,192,384]{3,2,1,0:T(8,128)(2,1)} %get-tuple-element.107), channel_id=1, source_target_pairs={{0,16},{16,0},{1,17},{17,1},{2,18},{18,2},{3,19},{19,3},{4,20},{20... | collective-permute-start | bytes 3538952 | tf_op jit(solution)/shard_map/ppermute | solution.py:639
  202.4 63.6 %collective-permute-start.48 = (bf16[2,4,48,1536]{3,2,1,0:T(8,128)(2,1)}, bf16[2,4,48,1536]{3,2,1,0:T(8,128)(2,1)}, u32[]{:S(2)}, u32[]{:S(2)}) collective-permute-start(bf16[2,4,48,1536]{3,2,1,0:T(8,128)(2,1)} %get-tuple-element.99), channel_id=1, source_target_pairs={{0,16},{16,0},{1,17},{17,1},{2,18},{18,2},{3,19},{19,3},{4,20},{20... | collective-permute-start | bytes 3538952 | tf_op jit(solution)/shard_map/ppermute | solution.py:639
  244.1 62.2 %collective-permute-start.15 = (bf16[256,5376]{1,0:T(8,128)(2,1)S(1)}, bf16[256,5376]{1,0:T(8,128)(2,1)S(1)}, u32[]{:S(2)}, u32[]{:S(2)}) collective-permute-start(bf16[256,5376]{1,0:T(8,128)(2,1)S(1)} %copy-done), channel_id=1, source_target_pairs={{0,1},{1,0},{2,3},{3,2},{4,5},{5,4},{6,7},{7,6},{8,9},{9,8},{10,11... | collective-permute-start | bytes 8257544 | tf_op jit(solution)/shard_map/ppermute | solution.py:647
  249.0 39.9 %collective-permute-start.49 = (bf16[2,4,48,1536]{3,2,1,0:T(8,128)(2,1)}, bf16[2,4,48,1536]{3,2,1,0:T(8,128)(2,1)}, u32[]{:S(2)}, u32[]{:S(2)}) collective-permute-start(bf16[2,4,48,1536]{3,2,1,0:T(8,128)(2,1)} %get-tuple-element.100), channel_id=1, source_target_pairs={{0,16},{16,0},{1,17},{17,1},{2,18},{18,2},{3,19},{19,3},{4,20},{20... | collective-permute-start | bytes 3538952 | tf_op jit(solution)/shard_map/ppermute | solution.py:639
  249.8 53.1 %collective-permute-start.6 = (bf16[1024,768]{1,0:T(8,128)(2,1)}, bf16[1024,768]{1,0:T(8,128)(2,1)}, u32[]{:S(2)}, u32[]{:S(2)}) collective-permute-start(bf16[1024,768]{1,0:T(8,128)(2,1)} %get-tuple-element.61), channel_id=1, source_target_pairs={{0,16},{16,0},{1,17},{17,1},{2,18},{18,2},{3,19},{19,3},{4,20},{20... | collective-permute-start | bytes 4718600 | tf_op jit(solution)/shard_map/ppermute | solution.py:639
  258.5 39.9 %collective-permute-start.24 = (bf16[2,4,48,1152]{3,2,1,0:T(8,128)(2,1)}, bf16[2,4,48,1152]{3,2,1,0:T(8,128)(2,1)}, u32[]{:S(2)}, u32[]{:S(2)}) collective-permute-start(bf16[2,4,48,1152]{3,2,1,0:T(8,128)(2,1)} %get-tuple-element.87), channel_id=1, source_target_pairs={{0,1},{1,0},{2,3},{3,2},{4,5},{5,4},{6,7},{7,6},{8,9},{9,8},{10,11... | collective-permute-start | bytes 2654216 | tf_op jit(solution)/shard_map/ppermute | solution.py:645
  266.0 51.2 %collective-permute-start.16 = (bf16[256,3456]{1,0:T(8,128)(2,1)}, bf16[256,3456]{1,0:T(8,128)(2,1)S(1)}, u32[]{:S(2)}, u32[]{:S(2)}) collective-permute-start(bf16[256,3456]{1,0:T(8,128)(2,1)} %get-tuple-element.79), channel_id=1, source_target_pairs={{0,1},{1,0},{2,3},{3,2},{4,5},{5,4},{6,7},{7,6},{8,9},{9,8},{10,11... | collective-permute-start | bytes 5308424 | tf_op jit(solution)/shard_map/ppermute | solution.py:647
  288.9 64.8 %collective-permute-start.9 = (bf16[1024,768]{1,0:T(8,128)(2,1)}, bf16[1024,768]{1,0:T(8,128)(2,1)}, u32[]{:S(2)}, u32[]{:S(2)}) collective-permute-start(bf16[1024,768]{1,0:T(8,128)(2,1)} %input_grad.1), channel_id=1, source_target_pairs={{0,16},{16,0},{1,17},{17,1},{2,18},{18,2},{3,19},{19,3},{4,20},{20... | collective-permute-start | bytes 4718600 | tf_op jit(solution)/shard_map/ppermute | solution.py:639
  298.4 77.6 %collective-permute-start.50 = (bf16[2,4,48,1536]{3,2,1,0:T(8,128)(2,1)}, bf16[2,4,48,1536]{3,2,1,0:T(8,128)(2,1)}, u32[]{:S(2)}, u32[]{:S(2)}) collective-permute-start(bf16[2,4,48,1536]{3,2,1,0:T(8,128)(2,1)} %get-tuple-element.102), channel_id=1, source_target_pairs={{0,2},{1,3},{2,0},{3,1},{4,6},{5,7},{6,4},{7,5},{8,10},{9,11},{10,... | collective-permute-start | bytes 3538952 | tf_op jit(solution)/shard_map/ppermute | solution.py:645
  302.9 46.0 %collective-permute-start.25 = (bf16[4,48,1152]{2,1,0:T(8,128)(2,1)}, bf16[4,48,1152]{2,1,0:T(8,128)(2,1)}, u32[]{:S(2)}, u32[]{:S(2)}) collective-permute-start(bf16[4,48,1152]{2,1,0:T(8,128)(2,1)} %get-tuple-element.128), channel_id=1, source_target_pairs={{0,2},{1,3},{2,0},{3,1},{4,6},{5,7},{6,4},{7,5},{8,10},{9,11},{10,... | collective-permute-start | bytes 1327112 | tf_op jit(solution)/shard_map/ppermute | solution.py:645
  338.1 14.9 %collective-permute-start.30 = (bf16[2,4,48,384]{3,2,0,1:T(8,128)(2,1)S(1)}, bf16[2,4,48,384]{3,2,0,1:T(8,128)(2,1)S(1)}, u32[]{:S(2)}, u32[]{:S(2)}) collective-permute-start(bf16[2,4,48,384]{3,2,0,1:T(8,128)(2,1)S(1)} %copy.23), channel_id=1, source_target_pairs={{0,2},{1,3},{2,0},{3,1},{4,6},{5,7},{6,4},{7,5},{8,10},{9,11},{10,... | collective-permute-start | bytes 884744 | tf_op jit(solution)/shard_map/ppermute | solution.py:647
  350.0 11.2 %collective-permute-start.26 = (bf16[48,1152]{1,0:T(8,128)(2,1)S(1)}, bf16[48,1152]{1,0:T(8,128)(2,1)S(1)}, u32[]{:S(2)}, u32[]{:S(2)}) collective-permute-start(bf16[48,1152]{1,0:T(8,128)(2,1)S(1)} %get-tuple-element.138), channel_id=1, source_target_pairs={{0,4},{1,5},{2,6},{3,7},{4,0},{5,1},{6,2},{7,3},{8,12},{9,13},{10,... | collective-permute-start | bytes 331784 | tf_op jit(solution)/shard_map/ppermute | solution.py:645
  350.1 11.2 %collective-permute-start.27 = (bf16[48,1152]{1,0:T(8,128)(2,1)S(1)}, bf16[48,1152]{1,0:T(8,128)(2,1)S(1)}, u32[]{:S(2)}, u32[]{:S(2)}) collective-permute-start(bf16[48,1152]{1,0:T(8,128)(2,1)S(1)} %get-tuple-element.140), channel_id=1, source_target_pairs={{0,8},{1,9},{2,10},{3,11},{4,12},{5,13},{6,14},{7,15},{8,0},{9,1},... | collective-permute-start | bytes 331784 | tf_op jit(solution)/shard_map/ppermute | solution.py:645
  353.0 10.4 %collective-permute-start.28 = (bf16[48,1152]{1,0:T(8,128)(2,1)S(1)}, bf16[48,1152]{1,0:T(8,128)(2,1)S(1)}, u32[]{:S(2)}, u32[]{:S(2)}) collective-permute-start(bf16[48,1152]{1,0:T(8,128)(2,1)S(1)} %get-tuple-element.139), channel_id=1, source_target_pairs={{0,12},{1,13},{2,14},{3,15},{4,8},{5,9},{6,10},{7,11},{8,4},{9,5},... | collective-permute-start | bytes 331784 | tf_op jit(solution)/shard_map/ppermute | solution.py:645
  353.7 13.4 %collective-permute-start.31 = (bf16[2,48,384]{2,1,0:T(8,128)(2,1)S(1)}, bf16[2,48,384]{2,1,0:T(8,128)(2,1)S(1)}, u32[]{:S(2)}, u32[]{:S(2)}) collective-permute-start(bf16[2,48,384]{2,1,0:T(8,128)(2,1)S(1)} %get-tuple-element.143), channel_id=1, source_target_pairs={{0,4},{1,5},{2,6},{3,7},{4,0},{5,1},{6,2},{7,3},{8,12},{9,13},{10,... | collective-permute-start | bytes 221192 | tf_op jit(solution)/shard_map/ppermute | solution.py:647
  361.3 66.6 %collective-permute-start.10 = (bf16[2,4,192,768]{3,2,1,0:T(8,128)(2,1)S(1)}, bf16[2,4,192,768]{3,2,1,0:T(8,128)(2,1)S(1)}, u32[]{:S(2)}, u32[]{:S(2)}) collective-permute-start(bf16[2,4,192,768]{3,2,1,0:T(8,128)(2,1)S(1)} %copy-done.25), channel_id=1, source_target_pairs={{0,2},{1,3},{2,0},{3,1},{4,6},{5,7},{6,4},{7,5},{8,10},{9,11},{10,... | collective-permute-start | bytes 7077896 | tf_op jit(solution)/shard_map/ppermute | solution.py:645
  361.4 19.6 %collective-permute-start.63 = (bf16[2,4,192,384]{3,2,1,0:T(8,128)(2,1)S(1)}, bf16[2,4,192,384]{3,2,1,0:T(8,128)(2,1)S(1)}, u32[]{:S(2)}, u32[]{:S(2)}) collective-permute-start(bf16[2,4,192,384]{3,2,1,0:T(8,128)(2,1)S(1)} %copy-done.26), channel_id=1, source_target_pairs={{0,1},{1,0},{2,3},{3,2},{4,5},{5,4},{6,7},{7,6},{8,9},{9,8},{10,11... | collective-permute-start | bytes 3538952 | tf_op jit(solution)/shard_map/ppermute | solution.py:645
  363.3 7.3 %collective-permute-start.32 = (bf16[2,48,384]{2,1,0:T(8,128)(2,1)S(1)}, bf16[2,48,384]{2,1,0:T(8,128)(2,1)S(1)}, u32[]{:S(2)}, u32[]{:S(2)}) collective-permute-start(bf16[2,48,384]{2,1,0:T(8,128)(2,1)S(1)} %get-tuple-element.145), channel_id=1, source_target_pairs={{0,8},{1,9},{2,10},{3,11},{4,12},{5,13},{6,14},{7,15},{8,0},{9,1},... | collective-permute-start | bytes 221192 | tf_op jit(solution)/shard_map/ppermute | solution.py:647
  367.1 6.2 %collective-permute-start.33 = (bf16[2,48,384]{2,1,0:T(8,128)(2,1)S(1)}, bf16[2,48,384]{2,1,0:T(8,128)(2,1)S(1)}, u32[]{:S(2)}, u32[]{:S(2)}) collective-permute-start(bf16[2,48,384]{2,1,0:T(8,128)(2,1)S(1)} %get-tuple-element.144), channel_id=1, source_target_pairs={{0,12},{1,13},{2,14},{3,15},{4,8},{5,9},{6,10},{7,11},{8,4},{9,5},... | collective-permute-start | bytes 221192 | tf_op jit(solution)/shard_map/ppermute | solution.py:647
  370.7 19.2 %collective-permute-start.42 = (f32[48,384]{1,0:T(8,128)S(1)}, f32[48,384]{1,0:T(8,128)S(1)}, u32[]{:S(2)}, u32[]{:S(2)}) collective-permute-start(f32[48,384]{1,0:T(8,128)S(1)} %fusion.79), channel_id=1, source_target_pairs={{0,16},{16,0},{1,17},{17,1},{2,18},{18,2},{3,19},{19,3},{4,20},{20... | collective-permute-start | bytes 221192 | tf_op jit(solution)/shard_map/ppermute | solution.py:639
  373.4 100.2 %collective-permute-start.56 = (bf16[2,4,192,384]{3,2,0,1:T(8,128)(2,1)S(1)}, bf16[2,4,192,384]{3,2,0,1:T(8,128)(2,1)S(1)}, u32[]{:S(2)}, u32[]{:S(2)}) collective-permute-start(bf16[2,4,192,384]{3,2,0,1:T(8,128)(2,1)S(1)} %copy.33), channel_id=1, source_target_pairs={{0,2},{1,3},{2,0},{3,1},{4,6},{5,7},{6,4},{7,5},{8,10},{9,11},{10,... | collective-permute-start | bytes 3538952 | tf_op jit(solution)/shard_map/ppermute | solution.py:647
  376.0 49.8 %collective-permute-start.17 = (bf16[2,4,48,1152]{3,2,0,1:T(8,128)(2,1)S(1)}, bf16[2,4,48,1152]{3,2,0,1:T(8,128)(2,1)S(1)}, u32[]{:S(2)}, u32[]{:S(2)}) collective-permute-start(bf16[2,4,48,1152]{3,2,0,1:T(8,128)(2,1)S(1)} %copy.18), channel_id=1, source_target_pairs={{0,2},{1,3},{2,0},{3,1},{4,6},{5,7},{6,4},{7,5},{8,10},{9,11},{10,... | collective-permute-start | bytes 2654216 | tf_op jit(solution)/shard_map/ppermute | solution.py:647
  381.0 5.9 %collective-permute-start.34 = (bf16[48,384]{1,0:T(8,128)(2,1)S(1)}, bf16[48,384]{1,0:T(8,128)(2,1)S(1)}, u32[]{:S(2)}, u32[]{:S(2)}) collective-permute-start(bf16[48,384]{1,0:T(8,128)(2,1)S(1)} %fusion.83), channel_id=1, source_target_pairs={{0,1},{1,0},{2,3},{3,2},{4,5},{5,4},{6,7},{7,6},{8,9},{9,8},{10,11... | collective-permute-start | bytes 110600 | tf_op jit(solution)/shard_map/ppermute | solution.py:647
  386.9 86.3 %collective-permute-start.43 = (bf16[2,4,48,1536]{3,2,0,1:T(8,128)(2,1)S(1)}, bf16[2,4,48,1536]{3,2,0,1:T(8,128)(2,1)S(1)}, u32[]{:S(2)}, u32[]{:S(2)}) collective-permute-start(bf16[2,4,48,1536]{3,2,0,1:T(8,128)(2,1)S(1)} %copy.28), channel_id=1, source_target_pairs={{0,2},{1,3},{2,0},{3,1},{4,6},{5,7},{6,4},{7,5},{8,10},{9,11},{10,... | collective-permute-start | bytes 3538952 | tf_op jit(solution)/shard_map/ppermute | solution.py:647
  389.9 54.9 %collective-permute-start.64 = (bf16[4,192,384]{2,1,0:T(8,128)(2,1)S(1)}, bf16[4,192,384]{2,1,0:T(8,128)(2,1)S(1)}, u32[]{:S(2)}, u32[]{:S(2)}) collective-permute-start(bf16[4,192,384]{2,1,0:T(8,128)(2,1)S(1)} %get-tuple-element.115), channel_id=1, source_target_pairs={{0,2},{1,3},{2,0},{3,1},{4,6},{5,7},{6,4},{7,5},{8,10},{9,11},{10,... | collective-permute-start | bytes 1769480 | tf_op jit(solution)/shard_map/ppermute | solution.py:645
  425.8 9.9 %collective-permute-start.51 = (bf16[4,48,1536]{2,1,0:T(8,128)(2,1)S(1)}, bf16[4,48,1536]{2,1,0:T(8,128)(2,1)S(1)}, u32[]{:S(2)}, u32[]{:S(2)}) collective-permute-start(bf16[4,48,1536]{2,1,0:T(8,128)(2,1)S(1)} %get-tuple-element.120), channel_id=1, source_target_pairs={{0,1},{1,0},{2,3},{3,2},{4,5},{5,4},{6,7},{7,6},{8,9},{9,8},{10,11... | collective-permute-start | bytes 1769480 | tf_op jit(solution)/shard_map/ppermute | solution.py:645
  427.9 20.4 %collective-permute-start.18 = (bf16[2,48,1152]{2,1,0:T(8,128)(2,1)S(1)}, bf16[2,48,1152]{2,1,0:T(8,128)(2,1)S(1)}, u32[]{:S(2)}, u32[]{:S(2)}) collective-permute-start(bf16[2,48,1152]{2,1,0:T(8,128)(2,1)S(1)} %get-tuple-element.129), channel_id=1, source_target_pairs={{0,4},{1,5},{2,6},{3,7},{4,0},{5,1},{6,2},{7,3},{8,12},{9,13},{10,... | collective-permute-start | bytes 663560 | tf_op jit(solution)/shard_map/ppermute | solution.py:647
  435.6 14.0 %collective-permute-start.19 = (bf16[2,48,1152]{2,1,0:T(8,128)(2,1)S(1)}, bf16[2,48,1152]{2,1,0:T(8,128)(2,1)S(1)}, u32[]{:S(2)}, u32[]{:S(2)}) collective-permute-start(bf16[2,48,1152]{2,1,0:T(8,128)(2,1)S(1)} %get-tuple-element.131), channel_id=1, source_target_pairs={{0,8},{1,9},{2,10},{3,11},{4,12},{5,13},{6,14},{7,15},{8,0},{9,1},... | collective-permute-start | bytes 663560 | tf_op jit(solution)/shard_map/ppermute | solution.py:647
  444.7 10.2 %collective-permute-start.20 = (bf16[2,48,1152]{2,1,0:T(8,128)(2,1)S(1)}, bf16[2,48,1152]{2,1,0:T(8,128)(2,1)S(1)}, u32[]{:S(2)}, u32[]{:S(2)}) collective-permute-start(bf16[2,48,1152]{2,1,0:T(8,128)(2,1)S(1)} %get-tuple-element.130), channel_id=1, source_target_pairs={{0,12},{1,13},{2,14},{3,15},{4,8},{5,9},{6,10},{7,11},{8,4},{9,5},... | collective-permute-start | bytes 663560 | tf_op jit(solution)/shard_map/ppermute | solution.py:647
  448.3 8.2 %collective-permute-start.65 = (bf16[192,384]{1,0:T(8,128)(2,1)S(1)}, bf16[192,384]{1,0:T(8,128)(2,1)S(1)}, u32[]{:S(2)}, u32[]{:S(2)}) collective-permute-start(bf16[192,384]{1,0:T(8,128)(2,1)S(1)} %get-tuple-element.132), channel_id=1, source_target_pairs={{0,4},{1,5},{2,6},{3,7},{4,0},{5,1},{6,2},{7,3},{8,12},{9,13},{10,... | collective-permute-start | bytes 442376 | tf_op jit(solution)/shard_map/ppermute | solution.py:645
  449.7 7.8 %collective-permute-start.66 = (bf16[192,384]{1,0:T(8,128)(2,1)S(1)}, bf16[192,384]{1,0:T(8,128)(2,1)S(1)}, u32[]{:S(2)}, u32[]{:S(2)}) collective-permute-start(bf16[192,384]{1,0:T(8,128)(2,1)S(1)} %get-tuple-element.134), channel_id=1, source_target_pairs={{0,8},{1,9},{2,10},{3,11},{4,12},{5,13},{6,14},{7,15},{8,0},{9,1},... | collective-permute-start | bytes 442376 | tf_op jit(solution)/shard_map/ppermute | solution.py:645
  454.9 6.7 %collective-permute-start.67 = (bf16[192,384]{1,0:T(8,128)(2,1)S(1)}, bf16[192,384]{1,0:T(8,128)(2,1)S(1)}, u32[]{:S(2)}, u32[]{:S(2)}) collective-permute-start(bf16[192,384]{1,0:T(8,128)(2,1)S(1)} %get-tuple-element.133), channel_id=1, source_target_pairs={{0,12},{1,13},{2,14},{3,15},{4,8},{5,9},{6,10},{7,11},{8,4},{9,5},... | collective-permute-start | bytes 442376 | tf_op jit(solution)/shard_map/ppermute | solution.py:645
  456.5 6.6 %collective-permute-start.52 = (bf16[48,1536]{1,0:T(8,128)(2,1)S(1)}, bf16[48,1536]{1,0:T(8,128)(2,1)S(1)}, u32[]{:S(2)}, u32[]{:S(2)}) collective-permute-start(bf16[48,1536]{1,0:T(8,128)(2,1)S(1)} %get-tuple-element.135), channel_id=1, source_target_pairs={{0,4},{1,5},{2,6},{3,7},{4,0},{5,1},{6,2},{7,3},{8,12},{9,13},{10,... | collective-permute-start | bytes 442376 | tf_op jit(solution)/shard_map/ppermute | solution.py:645
  457.5 6.6 %collective-permute-start.53 = (bf16[48,1536]{1,0:T(8,128)(2,1)S(1)}, bf16[48,1536]{1,0:T(8,128)(2,1)S(1)}, u32[]{:S(2)}, u32[]{:S(2)}) collective-permute-start(bf16[48,1536]{1,0:T(8,128)(2,1)S(1)} %get-tuple-element.137), channel_id=1, source_target_pairs={{0,8},{1,9},{2,10},{3,11},{4,12},{5,13},{6,14},{7,15},{8,0},{9,1},... | collective-permute-start | bytes 442376 | tf_op jit(solution)/shard_map/ppermute | solution.py:645
  461.6 6.9 %collective-permute-start.54 = (bf16[48,1536]{1,0:T(8,128)(2,1)S(1)}, bf16[48,1536]{1,0:T(8,128)(2,1)S(1)}, u32[]{:S(2)}, u32[]{:S(2)}) collective-permute-start(bf16[48,1536]{1,0:T(8,128)(2,1)S(1)} %get-tuple-element.136), channel_id=1, source_target_pairs={{0,12},{1,13},{2,14},{3,15},{4,8},{5,9},{6,10},{7,11},{8,4},{9,5},... | collective-permute-start | bytes 442376 | tf_op jit(solution)/shard_map/ppermute | solution.py:645
  463.1 33.2 %collective-permute-start.29 = (f32[48,1152]{1,0:T(8,128)S(1)}, f32[48,1152]{1,0:T(8,128)S(1)}, u32[]{:S(2)}, u32[]{:S(2)}) collective-permute-start(f32[48,1152]{1,0:T(8,128)S(1)} %fusion.53), channel_id=1, source_target_pairs={{0,16},{16,0},{1,17},{17,1},{2,18},{18,2},{3,19},{19,3},{4,20},{20... | collective-permute-start | bytes 663560 | tf_op jit(solution)/shard_map/ppermute | solution.py:639
  464.1 83.8 %collective-permute-start.11 = (bf16[4,192,768]{2,1,0:T(8,128)(2,1)S(1)}, bf16[4,192,768]{2,1,0:T(8,128)(2,1)S(1)}, u32[]{:S(2)}, u32[]{:S(2)}) collective-permute-start(bf16[4,192,768]{2,1,0:T(8,128)(2,1)S(1)} %get-tuple-element.113), channel_id=1, source_target_pairs={{0,1},{1,0},{2,3},{3,2},{4,5},{5,4},{6,7},{7,6},{8,9},{9,8},{10,11... | collective-permute-start | bytes 3538952 | tf_op jit(solution)/shard_map/ppermute | solution.py:645
  468.5 24.3 %collective-permute-start.21 = (bf16[48,1152]{1,0:T(8,128)(2,1)S(1)}, bf16[48,1152]{1,0:T(8,128)(2,1)S(1)}, u32[]{:S(2)}, u32[]{:S(2)}) collective-permute-start(bf16[48,1152]{1,0:T(8,128)(2,1)S(1)} %fusion.69), channel_id=1, source_target_pairs={{0,1},{1,0},{2,3},{3,2},{4,5},{5,4},{6,7},{7,6},{8,9},{9,8},{10,11... | collective-permute-start | bytes 331784 | tf_op jit(solution)/shard_map/ppermute | solution.py:647
  473.2 73.8 %collective-permute-start.68 = (f32[192,384]{1,0:T(8,128)S(1)}, f32[192,384]{1,0:T(8,128)S(1)}, u32[]{:S(2)}, u32[]{:S(2)}) collective-permute-start(f32[192,384]{1,0:T(8,128)S(1)} %fusion.36), channel_id=1, source_target_pairs={{0,16},{16,0},{1,17},{17,1},{2,18},{18,2},{3,19},{19,3},{4,20},{20... | collective-permute-start | bytes 884744 | tf_op jit(solution)/shard_map/ppermute | solution.py:639
  473.6 26.7 %collective-permute-start.44 = (bf16[2,48,1536]{2,1,0:T(8,128)(2,1)S(1)}, bf16[2,48,1536]{2,1,0:T(8,128)(2,1)S(1)}, u32[]{:S(2)}, u32[]{:S(2)}) collective-permute-start(bf16[2,48,1536]{2,1,0:T(8,128)(2,1)S(1)} %get-tuple-element.121), channel_id=1, source_target_pairs={{0,4},{1,5},{2,6},{3,7},{4,0},{5,1},{6,2},{7,3},{8,12},{9,13},{10,... | collective-permute-start | bytes 884744 | tf_op jit(solution)/shard_map/ppermute | solution.py:647
  492.8 14.0 %collective-permute-start.45 = (bf16[2,48,1536]{2,1,0:T(8,128)(2,1)S(1)}, bf16[2,48,1536]{2,1,0:T(8,128)(2,1)S(1)}, u32[]{:S(2)}, u32[]{:S(2)}) collective-permute-start(bf16[2,48,1536]{2,1,0:T(8,128)(2,1)S(1)} %get-tuple-element.123), channel_id=1, source_target_pairs={{0,8},{1,9},{2,10},{3,11},{4,12},{5,13},{6,14},{7,15},{8,0},{9,1},... | collective-permute-start | bytes 884744 | tf_op jit(solution)/shard_map/ppermute | solution.py:647
  496.3 15.9 %collective-permute-start.46 = (bf16[2,48,1536]{2,1,0:T(8,128)(2,1)S(1)}, bf16[2,48,1536]{2,1,0:T(8,128)(2,1)S(1)}, u32[]{:S(2)}, u32[]{:S(2)}) collective-permute-start(bf16[2,48,1536]{2,1,0:T(8,128)(2,1)S(1)} %get-tuple-element.122), channel_id=1, source_target_pairs={{0,12},{1,13},{2,14},{3,15},{4,8},{5,9},{6,10},{7,11},{8,4},{9,5},... | collective-permute-start | bytes 884744 | tf_op jit(solution)/shard_map/ppermute | solution.py:647
  500.2 15.3 %collective-permute-start.57 = (bf16[2,192,384]{2,1,0:T(8,128)(2,1)S(1)}, bf16[2,192,384]{2,1,0:T(8,128)(2,1)S(1)}, u32[]{:S(2)}, u32[]{:S(2)}) collective-permute-start(bf16[2,192,384]{2,1,0:T(8,128)(2,1)S(1)} %get-tuple-element.116), channel_id=1, source_target_pairs={{0,4},{1,5},{2,6},{3,7},{4,0},{5,1},{6,2},{7,3},{8,12},{9,13},{10,... | collective-permute-start | bytes 884744 | tf_op jit(solution)/shard_map/ppermute | solution.py:647
  506.8 15.9 %collective-permute-start.58 = (bf16[2,192,384]{2,1,0:T(8,128)(2,1)S(1)}, bf16[2,192,384]{2,1,0:T(8,128)(2,1)S(1)}, u32[]{:S(2)}, u32[]{:S(2)}) collective-permute-start(bf16[2,192,384]{2,1,0:T(8,128)(2,1)S(1)} %get-tuple-element.118), channel_id=1, source_target_pairs={{0,8},{1,9},{2,10},{3,11},{4,12},{5,13},{6,14},{7,15},{8,0},{9,1},... | collective-permute-start | bytes 884744 | tf_op jit(solution)/shard_map/ppermute | solution.py:647
  512.2 24.1 %collective-permute-start.59 = (bf16[2,192,384]{2,1,0:T(8,128)(2,1)S(1)}, bf16[2,192,384]{2,1,0:T(8,128)(2,1)S(1)}, u32[]{:S(2)}, u32[]{:S(2)}) collective-permute-start(bf16[2,192,384]{2,1,0:T(8,128)(2,1)S(1)} %get-tuple-element.117), channel_id=1, source_target_pairs={{0,12},{1,13},{2,14},{3,15},{4,8},{5,9},{6,10},{7,11},{8,4},{9,5},... | collective-permute-start | bytes 884744 | tf_op jit(solution)/shard_map/ppermute | solution.py:647
  515.5 36.1 %collective-permute-start.55 = (f32[48,1536]{1,0:T(8,128)S(1)}, f32[48,1536]{1,0:T(8,128)S(1)}, u32[]{:S(2)}, u32[]{:S(2)}) collective-permute-start(f32[48,1536]{1,0:T(8,128)S(1)} %fusion.43), channel_id=1, source_target_pairs={{0,16},{16,0},{1,17},{17,1},{2,18},{18,2},{3,19},{19,3},{4,20},{20... | collective-permute-start | bytes 884744 | tf_op jit(solution)/shard_map/ppermute | solution.py:639
  536.5 7.0 %collective-permute-start.47 = (bf16[48,1536]{1,0:T(8,128)(2,1)S(1)}, bf16[48,1536]{1,0:T(8,128)(2,1)S(1)}, u32[]{:S(2)}, u32[]{:S(2)}) collective-permute-start(bf16[48,1536]{1,0:T(8,128)(2,1)S(1)} %fusion.61), channel_id=1, source_target_pairs={{0,1},{1,0},{2,3},{3,2},{4,5},{5,4},{6,7},{7,6},{8,9},{9,8},{10,11... | collective-permute-start | bytes 442376 | tf_op jit(solution)/shard_map/ppermute | solution.py:647
  539.9 7.0 %collective-permute-start.60 = (bf16[192,384]{1,0:T(8,128)(2,1)S(1)}, bf16[192,384]{1,0:T(8,128)(2,1)S(1)}, u32[]{:S(2)}, u32[]{:S(2)}) collective-permute-start(bf16[192,384]{1,0:T(8,128)(2,1)S(1)} %fusion.62), channel_id=1, source_target_pairs={{0,1},{1,0},{2,3},{3,2},{4,5},{5,4},{6,7},{7,6},{8,9},{9,8},{10,11... | collective-permute-start | bytes 442376 | tf_op jit(solution)/shard_map/ppermute | solution.py:647
  548.1 6.8 %collective-permute-start.12 = (bf16[192,768]{1,0:T(8,128)(2,1)S(1)}, bf16[192,768]{1,0:T(8,128)(2,1)S(1)}, u32[]{:S(2)}, u32[]{:S(2)}) collective-permute-start(bf16[192,768]{1,0:T(8,128)(2,1)S(1)} %get-tuple-element.124), channel_id=1, source_target_pairs={{0,4},{1,5},{2,6},{3,7},{4,0},{5,1},{6,2},{7,3},{8,12},{9,13},{10,... | collective-permute-start | bytes 884744 | tf_op jit(solution)/shard_map/ppermute | solution.py:645
  548.2 12.6 %collective-permute-start.13 = (bf16[192,768]{1,0:T(8,128)(2,1)S(1)}, bf16[192,768]{1,0:T(8,128)(2,1)S(1)}, u32[]{:S(2)}, u32[]{:S(2)}) collective-permute-start(bf16[192,768]{1,0:T(8,128)(2,1)S(1)} %get-tuple-element.126), channel_id=1, source_target_pairs={{0,8},{1,9},{2,10},{3,11},{4,12},{5,13},{6,14},{7,15},{8,0},{9,1},... | collective-permute-start | bytes 884744 | tf_op jit(solution)/shard_map/ppermute | solution.py:645
  550.1 15.8 %collective-permute-start.14 = (bf16[192,768]{1,0:T(8,128)(2,1)S(1)}, bf16[192,768]{1,0:T(8,128)(2,1)S(1)}, u32[]{:S(2)}, u32[]{:S(2)}) collective-permute-start(bf16[192,768]{1,0:T(8,128)(2,1)S(1)} %get-tuple-element.125), channel_id=1, source_target_pairs={{0,12},{1,13},{2,14},{3,15},{4,8},{5,9},{6,10},{7,11},{8,4},{9,5},... | collective-permute-start | bytes 884744 | tf_op jit(solution)/shard_map/ppermute | solution.py:645
  (36 other events, 457.4 us)
